TPU v7x, 32 devices: a whole 2x2x4 slice. The times are simulated.
32 devices in a mesh: ctx: 16 (over z, y, x), fsdp: 2 (over core).
Axes of the slice: x: 2, y: 2, z: 4, core: 2. Of those that a mesh axis runs over, the one named last changes fastest.
Arguments:
- hidden_in: bfloat16 [2, 16, 2, 246, 768], P('fsdp', 'ctx'), may hold values from -6 to 6
- read_memory: bfloat16 [2, 16, 2, 10, 768], P('fsdp', 'ctx'), may hold values from -6 to 6
- doc_ids: int32 [2, 8192], P('fsdp'), may hold values from 0 to 63, never falling along the last dimension, each value on 1 to 1024 neighbouring positions
- cotangent: bfloat16 [2, 16, 2, 256, 768], P('fsdp', 'ctx'), may hold values from -6 to 6
- in_weight: bfloat16 [2, 768, 2304], P(None, 'fsdp'), may hold values from -0.21875 to 0.21875
- in_bias: bfloat16 [2, 1536], P(None, 'fsdp'), may hold values from -1.5 to 1.5
- out_weight: bfloat16 [2, 768, 768], P(None, 'fsdp'), may hold values from -0.875 to 0.875
- out_bias: bfloat16 [2, 768], P(None, 'fsdp'), may hold values from -1.5 to 1.5
- gain_one: bfloat16 [2, 768], P(None, 'fsdp'), may hold values from 0.5 to 1.5
- shift_one: bfloat16 [2, 768], P(None, 'fsdp'), may hold values from -1.5 to 1.5
- up_weight: bfloat16 [2, 768, 3072], P(None, 'fsdp'), may hold values from -0.21875 to 0.21875
- up_bias: bfloat16 [2, 3072], P(None, 'fsdp'), may hold values from -2.5 to 2.5
- down_weight: bfloat16 [2, 3072, 768], P(None, 'fsdp'), may hold values from -0.109375 to 0.109375
- down_bias: bfloat16 [2, 768], P(None, 'fsdp'), may hold values from -1.5 to 1.5
- gain_two: bfloat16 [2, 768], P(None, 'fsdp'), may hold values from 0.5 to 1.5
- shift_two: bfloat16 [2, 768], P(None, 'fsdp'), may hold values from -1.5 to 1.5
Outputs:
- activations: bfloat16 [2, 16, 2, 256, 768], P('fsdp', 'ctx')
- new_memory: bfloat16 [2, 16, 2, 10, 768], P('fsdp', 'ctx')
- input_grad: bfloat16 [2, 16, 2, 246, 768], P('fsdp', 'ctx')
- memory_grad: bfloat16 [2, 16, 2, 10, 768], P('fsdp', 'ctx')
- in_weight_grad: float32 [2, 768, 2304], P(None, 'fsdp')
- in_bias_grad: float32 [2, 1536], P(None, 'fsdp')
- out_weight_grad: float32 [2, 768, 768], P(None, 'fsdp')
- out_bias_grad: float32 [2, 768], P(None, 'fsdp')
- gain_one_grad: float32 [2, 768], P(None, 'fsdp')
- shift_one_grad: float32 [2, 768], P(None, 'fsdp')
- up_weight_grad: float32 [2, 768, 3072], P(None, 'fsdp')
- up_bias_grad: float32 [2, 3072], P(None, 'fsdp')
- down_weight_grad: float32 [2, 3072, 768], P(None, 'fsdp')
- down_bias_grad: float32 [2, 768], P(None, 'fsdp')
- gain_two_grad: float32 [2, 768], P(None, 'fsdp')
- shift_two_grad: float32 [2, 768], P(None, 'fsdp')
Inputs may be any that keep to these rules, and one draw needn't show every extreme that they name: `doc_ids`: document numbers never fall along a sequence; each document holds 1 to min(1024, 2048) rows, one exactly that many.
All inputs are finite; a program needn't handle non-finite values.
Results may differ from a plain program's by a relative error of at most 0.024.
Values may be sent and summed in bfloat16 or wider, within the bound.
A program may use at most 320 MiB of HBM per device.

v0:
```python
import math

import jax
import jax.numpy as jnp
from jax import lax
from jax.sharding import PartitionSpec as P

HEAD_DIM = 64


EPSILON = 1e-06
NEGATIVE = -1e30
score_block = 512
inverse_root = 0.7071067811865476


def from_behind(x, axis, by):
    length = lax.axis_size(axis)
    pairs = [(i, i + by) for i in range(length) if 0 <= i + by < length]
    return lax.ppermute(x, axis, pairs)


def layer_norm(inputs, norm_gain, norm_shift):
    row_mean = jnp.mean(inputs, axis=-1, keepdims=True)
    centred = inputs - row_mean
    spread = jnp.mean(centred * centred, axis=-1, keepdims=True)
    return centred * lax.rsqrt(spread + EPSILON) * norm_gain + norm_shift


def gelu_exact(values):
    return 0.5 * values * (1.0 + lax.erf(values * inverse_root))


def rounded(values):
    return values.astype(jnp.bfloat16)


def unchanged(current_state):
    return current_state


def key_places(row_total, seg_rows, contexts):
    row_index = jnp.arange(row_total, dtype=jnp.int32)
    device = row_index // (2 * seg_rows)
    second = row_index // seg_rows % 2
    block_index = jnp.where(second == 0, device, 2 * contexts - 1 - device)
    return block_index * seg_rows + row_index % seg_rows


def visible_mask(key_pos, key_doc, query_pos, query_doc):
    return (key_doc[None, :] == query_doc[:, None]) & (key_pos[None, :] <= query_pos[:, None])


def masked_scores(query_rows, keys_rows, visible):
    scores = jnp.einsum("qhd,khd->hqk", query_rows, keys_rows, preferred_element_type=jnp.float32)
    return jnp.where(visible[None], scores, NEGATIVE)


def log_totals(queries, key_blocks, kpos_blocks, kdoc_blocks, query_pos, query_doc):
    head_count = queries.shape[1]
    query_rows = queries.shape[0]

    def log_step(carried, members):
        keys_block, key_pos, key_doc = members
        visible = visible_mask(key_pos, key_doc, query_pos, query_doc)

        def log_update(current_state):
            peak_old, total_old = current_state
            scores = masked_scores(queries, keys_block, visible)
            peak_new = jnp.maximum(peak_old, jnp.max(scores, axis=-1))
            total_new = total_old * jnp.exp(peak_old - peak_new) + jnp.sum(
                jnp.exp(scores - peak_new[:, :, None]), axis=-1
            )
            return (peak_new, total_new)

        return (lax.cond(jnp.any(visible), log_update, unchanged, carried), None)

    start_state = (
        jnp.full((head_count, query_rows), NEGATIVE, jnp.float32),
        jnp.zeros((head_count, query_rows), jnp.float32),
    )
    (running_peak, running_total), unused = lax.scan(
        log_step, start_state, (key_blocks, kpos_blocks, kdoc_blocks)
    )
    return running_peak + jnp.log(running_total)


def attend(
    queries, log_norm, key_blocks, value_blocks, kpos_blocks, kdoc_blocks, query_pos, query_doc
):

    def attend_step(carried, members):
        keys_block, values_block, key_pos, key_doc = members
        visible = visible_mask(key_pos, key_doc, query_pos, query_doc)

        def attend_update(current_state):
            scores = masked_scores(queries, keys_block, visible)
            weights_soft = rounded(jnp.exp(scores - log_norm[:, :, None]))
            return current_state + jnp.einsum(
                "hqk,khd->qhd", weights_soft, values_block, preferred_element_type=jnp.float32
            )

        return (lax.cond(jnp.any(visible), attend_update, unchanged, carried), None)

    start_state = jnp.zeros(queries.shape, jnp.float32)
    result, unused = lax.scan(
        attend_step, start_state, (key_blocks, value_blocks, kpos_blocks, kdoc_blocks)
    )
    return result


def query_grads(
    queries,
    grad_attended,
    log_norm,
    row_delta,
    key_blocks,
    value_blocks,
    kpos_blocks,
    kdoc_blocks,
    query_pos,
    query_doc,
):

    def query_step(carried, members):
        keys_block, values_block, key_pos, key_doc = members
        visible = visible_mask(key_pos, key_doc, query_pos, query_doc)

        def query_update(current_state):
            scores = masked_scores(queries, keys_block, visible)
            weights_soft = jnp.exp(scores - log_norm[:, :, None])
            grad_soft = jnp.einsum(
                "qhd,khd->hqk", grad_attended, values_block, preferred_element_type=jnp.float32
            )
            grad_scores = rounded(weights_soft * (grad_soft - row_delta[:, :, None]))
            return current_state + jnp.einsum(
                "hqk,khd->qhd", grad_scores, keys_block, preferred_element_type=jnp.float32
            )

        return (lax.cond(jnp.any(visible), query_update, unchanged, carried), None)

    start_state = jnp.zeros(queries.shape, jnp.float32)
    result, unused = lax.scan(
        query_step, start_state, (key_blocks, value_blocks, kpos_blocks, kdoc_blocks)
    )
    return result


def key_grads(
    keys_rows,
    values_rows,
    rows_pos,
    rows_doc,
    query_blocks,
    grad_blocks,
    norm_blocks,
    delta_blocks,
    qpos_blocks,
    qdoc_blocks,
):

    def key_step(carried, members):
        query_rows, grad_rows, norm_rows, delta_rows, qpos_rows, qdoc_rows = members
        visible = visible_mask(rows_pos, rows_doc, qpos_rows, qdoc_rows)

        def key_update(current_state):
            scores = masked_scores(query_rows, keys_rows, visible)
            weights_soft = jnp.exp(scores - norm_rows[:, :, None])
            grad_soft = jnp.einsum(
                "qhd,khd->hqk", grad_rows, values_rows, preferred_element_type=jnp.float32
            )
            grad_scores = rounded(weights_soft * (grad_soft - delta_rows[:, :, None]))
            grad_keys = current_state[0] + jnp.einsum(
                "hqk,qhd->khd", grad_scores, query_rows, preferred_element_type=jnp.float32
            )
            grad_values = current_state[1] + jnp.einsum(
                "hqk,qhd->khd", rounded(weights_soft), grad_rows, preferred_element_type=jnp.float32
            )
            return (grad_keys, grad_values)

        return (lax.cond(jnp.any(visible), key_update, unchanged, carried), None)

    start_state = (
        jnp.zeros(keys_rows.shape, jnp.float32),
        jnp.zeros(values_rows.shape, jnp.float32),
    )
    result, unused = lax.scan(
        key_step,
        start_state,
        (query_blocks, grad_blocks, norm_blocks, delta_blocks, qpos_blocks, qdoc_blocks),
    )
    return result


def left_product(left_rows, right_rows):
    return lax.dot_general(
        left_rows, right_rows, (((0,), (0,)), ((), ())), preferred_element_type=jnp.float32
    )


def right_product(left_rows, right_rows):
    return lax.dot_general(
        left_rows, right_rows, (((1,), (1,)), ((), ())), preferred_element_type=jnp.float32
    )


def local(
    hidden_in,
    read_memory,
    doc_ids,
    cotangent,
    in_weight,
    in_bias,
    out_weight,
    out_bias,
    gain_one,
    shift_one,
    up_weight,
    up_bias,
    down_weight,
    down_bias,
    gain_two,
    shift_two,
):
    model_width = hidden_in.shape[-1]
    seg_rows = cotangent.shape[3]
    mem_rows = read_memory.shape[3]
    local_rows = 2 * seg_rows
    head_count = model_width // HEAD_DIM
    contexts = lax.axis_size("ctx")
    own_index = lax.axis_index("ctx")
    documents = doc_ids[0]
    offsets = jnp.arange(seg_rows, dtype=jnp.int32)
    own_blocks = jnp.stack([own_index, 2 * contexts - 1 - own_index])
    query_pos = (own_blocks[:, None] * seg_rows + offsets[None, :]).reshape(local_rows)
    query_doc = documents[query_pos]
    gathered_rows = contexts * local_rows
    key_count = gathered_rows // score_block
    key_pos = key_places(gathered_rows, seg_rows, contexts)
    key_doc = documents[key_pos]
    kpos_blocks = key_pos.reshape(key_count, score_block)
    kdoc_blocks = key_doc.reshape(key_count, score_block)

    def forward_layer(inputs, layer_index):
        weights = (
            lax.all_gather(in_weight[layer_index], "fsdp", axis=0, tiled=True),
            lax.all_gather(in_bias[layer_index], "fsdp", axis=0, tiled=True),
            lax.all_gather(out_weight[layer_index], "fsdp", axis=0, tiled=True),
            lax.all_gather(out_bias[layer_index], "fsdp", axis=0, tiled=True),
            lax.all_gather(gain_one[layer_index], "fsdp", axis=0, tiled=True),
            lax.all_gather(shift_one[layer_index], "fsdp", axis=0, tiled=True),
            lax.all_gather(up_weight[layer_index], "fsdp", axis=0, tiled=True),
            lax.all_gather(up_bias[layer_index], "fsdp", axis=0, tiled=True),
            lax.all_gather(down_weight[layer_index], "fsdp", axis=0, tiled=True),
            lax.all_gather(down_bias[layer_index], "fsdp", axis=0, tiled=True),
            lax.all_gather(gain_two[layer_index], "fsdp", axis=0, tiled=True),
            lax.all_gather(shift_two[layer_index], "fsdp", axis=0, tiled=True),
        )
        (
            mixing_weight,
            mixing_bias,
            output_weight,
            output_bias,
            first_gain,
            first_shift,
            expand_weight,
            expand_bias,
            reduce_weight,
            reduce_bias,
            second_gain,
            second_shift,
        ) = weights
        low_inputs = rounded(inputs)
        zeros_mid = jnp.zeros((model_width,), jnp.float32)
        bias_all = jnp.concatenate(
            [
                mixing_bias[:model_width].astype(jnp.float32),
                zeros_mid,
                mixing_bias[model_width:].astype(jnp.float32),
            ]
        )
        mixed_rows = rounded(
            jnp.dot(low_inputs, mixing_weight, preferred_element_type=jnp.float32) + bias_all
        )
        queries = (mixed_rows[:, :model_width] * 0.125).reshape(local_rows, head_count, HEAD_DIM)
        all_keys, all_values = (
            lax.all_gather(mixed_rows[:, model_width : 2 * model_width], "ctx", axis=0, tiled=True),
            lax.all_gather(mixed_rows[:, 2 * model_width :], "ctx", axis=0, tiled=True),
        )
        key_blocks = all_keys.reshape(key_count, score_block, head_count, HEAD_DIM)
        value_blocks = all_values.reshape(key_count, score_block, head_count, HEAD_DIM)
        log_norm = log_totals(queries, key_blocks, kpos_blocks, kdoc_blocks, query_pos, query_doc)
        attended = attend(
            queries,
            log_norm,
            key_blocks,
            value_blocks,
            kpos_blocks,
            kdoc_blocks,
            query_pos,
            query_doc,
        )
        attended_low = rounded(attended.reshape(local_rows, model_width))
        first_sum = inputs + (
            jnp.dot(attended_low, output_weight, preferred_element_type=jnp.float32)
            + output_bias.astype(jnp.float32)
        )
        middle = layer_norm(
            first_sum, first_gain.astype(jnp.float32), first_shift.astype(jnp.float32)
        )
        middle_low = rounded(middle)
        hidden = jnp.dot(
            middle_low, expand_weight, preferred_element_type=jnp.float32
        ) + expand_bias.astype(jnp.float32)
        active = rounded(gelu_exact(hidden))
        second_sum = middle + (
            jnp.dot(active, reduce_weight, preferred_element_type=jnp.float32)
            + reduce_bias.astype(jnp.float32)
        )
        output = layer_norm(
            second_sum, second_gain.astype(jnp.float32), second_shift.astype(jnp.float32)
        )
        saved_state = (
            weights,
            low_inputs,
            mixed_rows,
            queries,
            all_keys,
            all_values,
            log_norm,
            attended,
            attended_low,
            first_sum,
            middle_low,
            hidden,
            active,
            second_sum,
        )
        return (output, saved_state)

    def backward_layer(grad_output, saved_state):
        (
            weights,
            low_inputs,
            mixed_rows,
            queries,
            all_keys,
            all_values,
            log_norm,
            attended,
            attended_low,
            first_sum,
            middle_low,
            hidden,
            active,
            second_sum,
        ) = saved_state
        (
            mixing_weight,
            mixing_bias,
            output_weight,
            output_bias,
            first_gain,
            first_shift,
            expand_weight,
            expand_bias,
            reduce_weight,
            reduce_bias,
            second_gain,
            second_shift,
        ) = weights
        unused, pull_second = jax.vjp(
            layer_norm,
            second_sum,
            second_gain.astype(jnp.float32),
            second_shift.astype(jnp.float32),
        )
        grad_second, grad_gain_two, grad_shift_two = pull_second(grad_output)
        grad_branch = rounded(grad_second)
        grad_reduce_bias = jnp.sum(grad_branch.astype(jnp.float32), axis=0)
        grad_reduce_weight = left_product(active, grad_branch)
        grad_active = right_product(grad_branch, reduce_weight)
        unused, pull_gelu = jax.vjp(gelu_exact, hidden)
        grad_hidden = rounded(pull_gelu(grad_active)[0])
        grad_expand_bias = jnp.sum(grad_hidden.astype(jnp.float32), axis=0)
        grad_expand_weight = left_product(middle_low, grad_hidden)
        grad_middle = grad_second + right_product(grad_hidden, expand_weight)
        unused, pull_first = jax.vjp(
            layer_norm, first_sum, first_gain.astype(jnp.float32), first_shift.astype(jnp.float32)
        )
        grad_first, grad_gain_one, grad_shift_one = pull_first(grad_middle)
        grad_attn_branch = rounded(grad_first)
        grad_output_bias = jnp.sum(grad_attn_branch.astype(jnp.float32), axis=0)
        grad_output_weight = left_product(attended_low, grad_attn_branch)
        grad_attended = rounded(right_product(grad_attn_branch, output_weight)).reshape(
            local_rows, head_count, HEAD_DIM
        )
        row_delta = jnp.einsum("qhd,qhd->hq", grad_attended.astype(jnp.float32), attended)
        key_blocks = all_keys.reshape(key_count, score_block, head_count, HEAD_DIM)
        value_blocks = all_values.reshape(key_count, score_block, head_count, HEAD_DIM)
        grad_queries = query_grads(
            queries,
            grad_attended,
            log_norm,
            row_delta,
            key_blocks,
            value_blocks,
            kpos_blocks,
            kdoc_blocks,
            query_pos,
            query_doc,
        )
        row_count = lax.axis_size("ctx") * local_rows
        piece_rows = math.gcd(row_count, score_block)
        pieces = row_count // piece_rows
        keys_part = all_keys.reshape(pieces, piece_rows, head_count, HEAD_DIM)
        values_part = all_values.reshape(pieces, piece_rows, head_count, HEAD_DIM)
        part_pos = key_places(row_count, seg_rows, contexts)
        part_doc = documents[part_pos]

        def one_piece(members):
            keys_rows, values_rows, rows_pos, rows_doc = members
            piece_keys, piece_values = key_grads(
                keys_rows,
                values_rows,
                rows_pos,
                rows_doc,
                queries[None],
                grad_attended[None],
                log_norm[None],
                row_delta[None],
                query_pos[None],
                query_doc[None],
            )
            return jnp.concatenate(
                [
                    piece_keys.reshape(piece_rows, model_width),
                    piece_values.reshape(piece_rows, model_width),
                ],
                axis=1,
            )

        key_terms = lax.psum_scatter(
            lax.map(
                one_piece,
                (
                    keys_part,
                    values_part,
                    part_pos.reshape(pieces, piece_rows),
                    part_doc.reshape(pieces, piece_rows),
                ),
            )
            .reshape(row_count, 2 * model_width)
            .astype(jnp.bfloat16),
            "ctx",
            scatter_dimension=0,
            tiled=True,
        ).astype(jnp.float32)
        grad_keys = key_terms[:, :model_width]
        grad_values = key_terms[:, model_width:]
        grad_mixed = rounded(
            jnp.concatenate(
                [grad_queries.reshape(local_rows, model_width) * 0.125, grad_keys, grad_values],
                axis=1,
            )
        )
        column_sums = jnp.sum(grad_mixed.astype(jnp.float32), axis=0)
        grad_mixing_bias = jnp.concatenate(
            [column_sums[:model_width], column_sums[2 * model_width :]]
        )
        grad_mixing_weight = left_product(low_inputs, grad_mixed)
        grad_inputs = grad_first + right_product(grad_mixed, mixing_weight)
        shards = (
            lax.psum_scatter(
                grad_mixing_weight.astype(jnp.bfloat16), "fsdp", scatter_dimension=0, tiled=True
            ).astype(jnp.float32),
            lax.psum_scatter(
                grad_mixing_bias.astype(jnp.bfloat16), "fsdp", scatter_dimension=0, tiled=True
            ).astype(jnp.float32),
            lax.psum_scatter(
                grad_output_weight.astype(jnp.bfloat16), "fsdp", scatter_dimension=0, tiled=True
            ).astype(jnp.float32),
            lax.psum_scatter(
                grad_output_bias.astype(jnp.bfloat16), "fsdp", scatter_dimension=0, tiled=True
            ).astype(jnp.float32),
            lax.psum_scatter(
                grad_gain_one.astype(jnp.bfloat16), "fsdp", scatter_dimension=0, tiled=True
            ).astype(jnp.float32),
            lax.psum_scatter(
                grad_shift_one.astype(jnp.bfloat16), "fsdp", scatter_dimension=0, tiled=True
            ).astype(jnp.float32),
            lax.psum_scatter(
                grad_expand_weight.astype(jnp.bfloat16), "fsdp", scatter_dimension=0, tiled=True
            ).astype(jnp.float32),
            lax.psum_scatter(
                grad_expand_bias.astype(jnp.bfloat16), "fsdp", scatter_dimension=0, tiled=True
            ).astype(jnp.float32),
            lax.psum_scatter(
                grad_reduce_weight.astype(jnp.bfloat16), "fsdp", scatter_dimension=0, tiled=True
            ).astype(jnp.float32),
            lax.psum_scatter(
                grad_reduce_bias.astype(jnp.bfloat16), "fsdp", scatter_dimension=0, tiled=True
            ).astype(jnp.float32),
            lax.psum_scatter(
                grad_gain_two.astype(jnp.bfloat16), "fsdp", scatter_dimension=0, tiled=True
            ).astype(jnp.float32),
            lax.psum_scatter(
                grad_shift_two.astype(jnp.bfloat16), "fsdp", scatter_dimension=0, tiled=True
            ).astype(jnp.float32),
        )
        summed = (
            lax.psum(shards[0].astype(jnp.bfloat16), "ctx").astype(jnp.float32),
            lax.psum(shards[1].astype(jnp.bfloat16), "ctx").astype(jnp.float32),
            lax.psum(shards[2].astype(jnp.bfloat16), "ctx").astype(jnp.float32),
            lax.psum(shards[3].astype(jnp.bfloat16), "ctx").astype(jnp.float32),
            lax.psum(shards[4].astype(jnp.bfloat16), "ctx").astype(jnp.float32),
            lax.psum(shards[5].astype(jnp.bfloat16), "ctx").astype(jnp.float32),
            lax.psum(shards[6].astype(jnp.bfloat16), "ctx").astype(jnp.float32),
            lax.psum(shards[7].astype(jnp.bfloat16), "ctx").astype(jnp.float32),
            lax.psum(shards[8].astype(jnp.bfloat16), "ctx").astype(jnp.float32),
            lax.psum(shards[9].astype(jnp.bfloat16), "ctx").astype(jnp.float32),
            lax.psum(shards[10].astype(jnp.bfloat16), "ctx").astype(jnp.float32),
            lax.psum(shards[11].astype(jnp.bfloat16), "ctx").astype(jnp.float32),
        )
        return (grad_inputs, summed)

    first_input = (
        jnp.concatenate([read_memory[0, 0], hidden_in[0, 0]], axis=1)
        .astype(jnp.float32)
        .reshape(local_rows, model_width)
    )
    middle_out, saved_first = forward_layer(first_input, 0)
    final_out, saved_second = forward_layer(middle_out, 1)
    final_low = rounded(final_out).reshape(2, seg_rows, model_width)
    write_rows = final_low[:, seg_rows - mem_rows :]
    from_left = from_behind(write_rows[0], "ctx", 1)
    from_right = from_behind(write_rows[1], "ctx", -1)
    memory_first = jnp.where(own_index == 0, read_memory[0, 0, 0], from_left)
    memory_second = jnp.where(own_index == contexts - 1, write_rows[0], from_right)
    new_memory = jnp.stack([memory_first, memory_second])[None, None]
    grad_final = cotangent[0, 0].astype(jnp.float32).reshape(local_rows, model_width)
    grad_middle_out, grads_second = backward_layer(grad_final, saved_second)
    grad_first_in, grads_first = backward_layer(grad_middle_out, saved_first)
    grad_blocks = grad_first_in.reshape(2, seg_rows, model_width)
    input_grad = rounded(grad_blocks[:, mem_rows:])[None, None]
    read_grads = rounded(grad_blocks[:, :mem_rows])
    next_first = from_behind(read_grads[0], "ctx", -1)
    next_second = from_behind(read_grads[1], "ctx", 1)
    memory_grad_first = jnp.where(own_index == contexts - 1, read_grads[1], next_first)
    memory_grad = jnp.stack([memory_grad_first, next_second])[None, None]
    stacked = [
        jnp.stack([first_part, second_part])
        for first_part, second_part in zip(grads_first, grads_second)
    ]
    return (
        final_low[None, None],
        new_memory,
        input_grad,
        memory_grad,
        stacked[0],
        stacked[1],
        stacked[2],
        stacked[3],
        stacked[4],
        stacked[5],
        stacked[6],
        stacked[7],
        stacked[8],
        stacked[9],
        stacked[10],
        stacked[11],
    )


def solution(mesh):
    in_specs = (
        P("fsdp", "ctx", None, None, None),
        P("fsdp", "ctx", None, None, None),
        P("fsdp", None),
        P("fsdp", "ctx", None, None, None),
        P(None, "fsdp", None),
        P(None, "fsdp"),
        P(None, "fsdp", None),
        P(None, "fsdp"),
        P(None, "fsdp"),
        P(None, "fsdp"),
        P(None, "fsdp", None),
        P(None, "fsdp"),
        P(None, "fsdp", None),
        P(None, "fsdp"),
        P(None, "fsdp"),
        P(None, "fsdp"),
    )
    out_specs = (
        P("fsdp", "ctx", None, None, None),
        P("fsdp", "ctx", None, None, None),
        P("fsdp", "ctx", None, None, None),
        P("fsdp", "ctx", None, None, None),
        P(None, "fsdp", None),
        P(None, "fsdp"),
        P(None, "fsdp", None),
        P(None, "fsdp"),
        P(None, "fsdp"),
        P(None, "fsdp"),
        P(None, "fsdp", None),
        P(None, "fsdp"),
        P(None, "fsdp", None),
        P(None, "fsdp"),
        P(None, "fsdp"),
        P(None, "fsdp"),
    )
    return jax.shard_map(local, mesh=mesh, in_specs=in_specs, out_specs=out_specs, check_vma=False)
```

profile of v0, /device:TPU:0, one launch (start us, length us, event | category | flops | bytes accessed | tf_op | source)
XLA Modules:
  0.0 3103.1 jit_solution(12155198653896521970)
XLA Ops:
  61.8 45.5 %gather_fusion = s32[8192]{0:T(1024)S(1)} fusion(s32[8192]{0:T(1024)S(1)} %bitcast.540, s32[8192]{0:T(1024)S(1)} %broadcast_clamp_fusion), kind=kCustom, calls=%fused_computation | custom fusion | bytes 98304 | tf_op jit(solution)/shard_map/gather | solution.py:240
  107.6 78.0 %all-gather.39.cloned.1.call-done = bf16[8192,768]{1,0:T(8,128)(2,1)} async-done(((bf16[512,768]{1,0:T(8,128)(2,1)}), bf16[8192,768]{1,0:T(8,128)(2,1)}) %all-gather.39.cloned.1.call-update) | async-done | bytes 12582928 | tf_op jit(solution)/shard_map/all_gather | solution.py:288
  185.7 16.8 copy.155
  211.9 18.6 copy.157
  230.6 108.7 %all-gather.37.cloned.1.call-done = bf16[8192,768]{1,0:T(8,128)(2,1)} async-done(((bf16[512,768]{1,0:T(8,128)(2,1)}), bf16[8192,768]{1,0:T(8,128)(2,1)}) %all-gather.37.cloned.1.call-update) | async-done | bytes 12582928 | tf_op jit(solution)/shard_map/all_gather | solution.py:287
  339.3 16.8 copy.152
  366.3 18.6 copy.156
  385.0 38.7 %while.114 = (s32[]{:T(128)}, f32[12,512]{1,0:T(8,128)S(1)}, f32[12,512]{1,0:T(8,128)S(1)}, s32[16,512]{1,0:T(8,128)S(1)}, s32[512]{0:T(512)S(1)}, /*index=5*/s3...) while((s32[]{:T(128)}, f32[12,512]{1,0:T(8,128)S(1)}, ...), condition=%wide.region_6.7_spmd.clone, body=%wide.region_0.6_spmd.clone.sunk | while | flops 419443200 | bytes 27867864 | solution.py:82
  424.5 38.0 %while.115 = (s32[]{:T(128)}, f32[512,12,64]{0,2,1:T(8,128)S(1)}, s32[16,512]{1,0:T(8,128)S(1)}, s32[512]{0:T(512)S(1)}, s32[16,512]{1,0:T(8,128)S(1)}, /*index=...) while((s32[]{:T(128)}, f32[512,12,64]{0,2,1:T(8,128)S(1)}, ...), condition=%wide.region_11.12_spmd.clone, body=%wide.region_7.11_spmd.clone.sunk | while | flops 816185856 | bytes 6085831 | solution.py:106
  504.5 196.9 %all-gather.43.cloned.1.call-done = bf16[8192,768]{1,0:T(8,128)(2,1)} async-done(((bf16[512,768]{1,0:T(8,128)(2,1)}), bf16[8192,768]{1,0:T(8,128)(2,1)}) %all-gather.43.cloned.1.call-update) | async-done | bytes 12582928 | tf_op jit(solution)/shard_map/all_gather | solution.py:288
  701.5 16.4 copy.161
  727.3 18.6 copy.163
  745.9 108.6 %all-gather.41.cloned.1.call-done = bf16[8192,768]{1,0:T(8,128)(2,1)} async-done(((bf16[512,768]{1,0:T(8,128)(2,1)}), bf16[8192,768]{1,0:T(8,128)(2,1)}) %all-gather.41.cloned.1.call-update) | async-done | bytes 12582928 | tf_op jit(solution)/shard_map/all_gather | solution.py:287
  854.5 16.7 copy.158
  881.1 18.6 copy.162
  899.7 38.5 %while.116 = (s32[]{:T(128)}, f32[12,512]{1,0:T(8,128)S(1)}, f32[12,512]{1,0:T(8,128)S(1)}, s32[16,512]{1,0:T(8,128)S(1)}, s32[512]{0:T(512)S(1)}, /*index=5*/s3...) while((s32[]{:T(128)}, f32[12,512]{1,0:T(8,128)S(1)}, ...), condition=%wide.region_22.23_spmd.clone, body=%wide.region_16.22_spmd.clone.sunk | while | flops 419443200 | bytes 27867864 | solution.py:82
  938.3 38.1 %while.117 = (s32[]{:T(128)}, f32[512,12,64]{0,2,1:T(8,128)S(1)}, s32[16,512]{1,0:T(8,128)S(1)}, s32[512]{0:T(512)S(1)}, s32[16,512]{1,0:T(8,128)S(1)}, /*index=...) while((s32[]{:T(128)}, f32[512,12,64]{0,2,1:T(8,128)S(1)}, ...), condition=%wide.region_27.28_spmd.clone, body=%wide.region_23.27_spmd.clone.sunk | while | flops 816185856 | bytes 6077639 | solution.py:106
  1026.0 208.5 %while.119 = (s32[]{:T(128)}, bf16[16,512,1536]{2,1,0:T(8,128)(2,1)}, s32[16,512]{1,0:T(8,128)S(1)}, s32[512]{0:T(512)S(1)}, s32[16,512]{1,0:T(8,128)S(1)}, /*in...) while((s32[]{:T(128)}, ...), condition=%wide.region_45.46_spmd.clone, body=%wide.region_41.45_spmd.clone.sunk | while | flops 1640759808 | bytes 71663440 | solution.py:444
  1028.9 27.0 conditional.29
  1045.0 10.8 bitcast_add_fusion.4
  1064.5 27.0 conditional.29
  1080.6 10.8 bitcast_add_fusion.4
  1235.9 66.8 %while.118 = (s32[]{:T(128)}, f32[512,12,64]{0,2,1:T(8,128)}, s32[16,512]{1,0:T(8,128)S(1)}, s32[512]{0:T(512)S(1)}, s32[16,512]{1,0:T(8,128)S(1)}, /*index=5*/b...) while((s32[]{:T(128)}, f32[512,12,64]{0,2,1:T(8,128)}, ...), condition=%wide.region_40.41_spmd.clone, body=%wide.region_36.40_spmd.clone.sunk | while | flops 1225130496 | bytes 32841448 | solution.py:143
  1238.1 19.1 conditional.28
  1245.6 11.6 bitcast_add_fusion.2
  1259.0 19.1 conditional.28
  1266.5 11.6 bitcast_add_fusion.2
  1307.8 504.1 %reduce-scatter.11.cloned.1.call-done = bf16[512,1536]{1,0:T(8,128)(2,1)} async-done(((bf16[8192,1536]{1,0:T(8,128)(2,1)}), bf16[512,1536]{1,0:T(8,128)(2,1)}) %reduce-scatter.11.cloned.1.call-update) | async-done | bytes 1572880 | tf_op jit(solution)/shard_map/reduce_scatter | solution.py:443
  1845.2 192.2 %while.121 = (s32[]{:T(128)}, bf16[16,512,1536]{2,1,0:T(8,128)(2,1)}, s32[16,512]{1,0:T(8,128)S(1)}, s32[512]{0:T(512)S(1)}, s32[16,512]{1,0:T(8,128)S(1)}, /*in...) while((s32[]{:T(128)}, ...), condition=%wide.region_60.61_spmd.clone, body=%wide.region_56.60_spmd.clone.sunk | while | flops 1640759808 | bytes 65380120 | solution.py:444
  1847.3 27.0 conditional.31
  1863.4 10.8 bitcast_add_fusion.7
  1881.8 27.0 conditional.31
  1898.0 10.8 bitcast_add_fusion.7
  2082.2 65.0 %while.120 = (s32[]{:T(128)}, f32[512,12,64]{0,2,1:T(8,128)}, s32[16,512]{1,0:T(8,128)S(1)}, s32[512]{0:T(512)S(1)}, s32[16,512]{1,0:T(8,128)S(1)}, /*index=5*/b...) while((s32[]{:T(128)}, f32[512,12,64]{0,2,1:T(8,128)}, ...), condition=%wide.region_55.56_spmd.clone, body=%wide.region_51.55_spmd.clone.sunk | while | flops 1225130496 | bytes 32849640 | solution.py:143
  2084.2 19.2 conditional.30
  2091.7 11.6 bitcast_add_fusion.5
  2104.9 19.2 conditional.30
  2112.5 11.6 bitcast_add_fusion.5
  2149.2 402.1 %reduce-scatter.13.cloned.1.call-done = bf16[512,1536]{1,0:T(8,128)(2,1)} async-done(((bf16[8192,1536]{1,0:T(8,128)(2,1)}), bf16[512,1536]{1,0:T(8,128)(2,1)}) %reduce-scatter.13.cloned.1.call-update) | async-done | bytes 1572880 | tf_op jit(solution)/shard_map/reduce_scatter | solution.py:443
  2561.1 16.7 reduce-scatter.25.cloned.1.call-done
  2577.7 16.5 reduce-scatter.29.cloned.1.call-done
  2594.2 12.0 reduce-scatter.19.cloned.1.call-done
  2606.3 14.9 reduce-scatter.17.cloned.1.call-done
  2621.2 16.6 reduce-scatter.23.cloned.1.call-done
  2637.8 16.1 reduce-scatter.27.cloned.1.call-done
  2653.9 14.9 reduce-scatter.15.cloned.1.call-done
  2694.5 84.9 %all-reduce.16 = (bf16[1,768]{1,0:T(2,128)(2,1)S(1)}, bf16[1,768]{1,0:T(2,128)(2,1)S(1)}, bf16[1,384]{1,0:T(2,128)(2,1)S(1)}, bf16[1,384]{1,0:T(2,128)(2,1)S(1)}...) all-reduce(bf16[1,768]{1,0:T(2,128)(2,1)S(1)} %stack.209, ...), channel_id=1, replica_groups=mesh['ctx'=16,'fsdp'=2] {'ctx'}, use_global_device_ids=true, to_apply=%region_71.72 | all-reduce | flops 9216 | bytes 36864 | tf_op jit(solution)/shard_map/psum | solution.py:513
  2789.2 290.5 %all-reduce.21.cloned.1.call-done = (bf16[1,384,2304]{2,1,0:T(8,128)(2,1)}, bf16[1,384,2304]{2,1,0:T(8,128)(2,1)}, bf16[1,384,768]{2,1,0:T(8,128)(2,1)}, bf16[1,...) async-done(((bf16[1,384,2304]{2,1,0:T(8,128)(2,1)}, ...) | async-done | bytes 14155792 | tf_op jit(solution)/shard_map/psum | solution.py:512
  (1391 shorter events, 914.1 us)
Async XLA Ops:
  7.2 51.5 %copy-start = (s32[1,8192]{1,0:T(1,128)S(1)}, s32[1,8192]{1,0:T(1,128)}, u32[]{:S(2)}) copy-start(s32[1,8192]{1,0:T(1,128)} %param.50) | copy-start | bytes 98308
  7.2 19.8 all-gather.45.cloned.1.call-start
  11.4 174.3 %all-gather.39.cloned.1.call-start = ((), (), s32[]{:S(2)}) async-start(), calls=%async_computation.11 | async-start | bytes 13369344 | tf_op jit(solution)/shard_map/all_gather | solution.py:288
  12.6 18.4 copy-start.37
  32.3 306.9 %all-gather.37.cloned.1.call-start = ((), (), s32[]{:S(2)}) async-start(), calls=%async_computation.10 | async-start | bytes 13369344 | tf_op jit(solution)/shard_map/all_gather | solution.py:287
  33.1 430.5 %all-gather.47.cloned.1.call-start = ((), (), s32[]{:S(2)}) async-start(), calls=%async_computation.25 | async-start | bytes 1769472 | tf_op jit(solution)/shard_map/all_gather | solution.py:248
  34.2 434.0 %all-gather.49.cloned.1.call-start = ((), (), s32[]{:S(2)}) async-start(), calls=%async_computation.26 | async-start | bytes 7077888 | tf_op jit(solution)/shard_map/all_gather | solution.py:252
  39.2 437.6 %all-gather.51.cloned.1.call-start = ((), (), s32[]{:S(2)}) async-start(), calls=%async_computation.27 | async-start | bytes 7077888 | tf_op jit(solution)/shard_map/all_gather | solution.py:254
  44.3 439.0 %all-gather.53.cloned.1.call-start = ((), (), s32[]{:S(2)}) async-start(), calls=%async_computation.28 | async-start | bytes 5308416 | tf_op jit(solution)/shard_map/all_gather | solution.py:246
  45.1 656.4 %all-gather.43.cloned.1.call-start = ((), (), s32[]{:S(2)}) async-start(), calls=%async_computation.13 | async-start | bytes 13369344 | tf_op jit(solution)/shard_map/all_gather | solution.py:288
  49.1 427.7 %copy-start.62 = (f32[768]{0:T(1024)}, f32[768]{0:T(1024)S(1)}, u32[]{:S(2)}) copy-start(f32[768]{0:T(1024)S(1)} %convert_reduce_fusion.10) | copy-start | bytes 9220
  51.0 425.9 %copy-start.94 = (f32[768]{0:T(1024)}, f32[768]{0:T(1024)S(1)}, u32[]{:S(2)}) copy-start(f32[768]{0:T(1024)S(1)} %convert_reduce_fusion.9) | copy-start | bytes 9220
  54.6 922.0 %copy-start.64 = (f32[768]{0:T(1024)}, f32[768]{0:T(1024)S(1)}, u32[]{:S(2)}) copy-start(f32[768]{0:T(1024)S(1)} %convert_reduce_fusion.7) | copy-start | bytes 9220
  56.5 920.1 %copy-start.96 = (f32[768]{0:T(1024)}, f32[768]{0:T(1024)S(1)}, u32[]{:S(2)}) copy-start(f32[768]{0:T(1024)S(1)} %convert_reduce_fusion.6) | copy-start | bytes 9220
  58.6 409.6 %copy-start.68 = (f32[1,3072]{1,0:T(1,128)}, f32[1,3072]{1,0:T(1,128)S(1)}, u32[]{:S(2)}) copy-start(f32[1,3072]{1,0:T(1,128)S(1)} %convert_element_type.421) | copy-start | bytes 36868
  482.9 493.7 %copy-start.54 = (f32[512]{0:T(512)}, f32[512]{0:T(512)S(1)}, u32[]{:S(2)}) copy-start(f32[512]{0:T(512)S(1)} %broadcast_multiply_fusion.2) | copy-start | bytes 6148
  483.3 493.4 %copy-start.78 = (f32[512]{0:T(512)}, f32[512]{0:T(512)S(1)}, u32[]{:S(2)}) copy-start(f32[512]{0:T(512)S(1)} %fusion.251) | copy-start | bytes 6148
  488.9 365.5 %all-gather.41.cloned.1.call-start = ((), (), s32[]{:S(2)}) async-start(), calls=%async_computation.12 | async-start | bytes 13369344 | tf_op jit(solution)/shard_map/all_gather | solution.py:287
  489.7 486.9 %all-gather.55.cloned.1.call-start = ((), (), s32[]{:S(2)}) async-start(), calls=%async_computation.29 | async-start | bytes 1769472 | tf_op jit(solution)/shard_map/all_gather | solution.py:248
  490.3 490.9 %all-gather.57.cloned.1.call-start = ((), (), s32[]{:S(2)}) async-start(), calls=%async_computation.30 | async-start | bytes 7077888 | tf_op jit(solution)/shard_map/all_gather | solution.py:252
  491.0 498.7 %all-gather.59.cloned.1.call-start = ((), (), s32[]{:S(2)}) async-start(), calls=%async_computation.31 | async-start | bytes 7077888 | tf_op jit(solution)/shard_map/all_gather | solution.py:254
  491.6 1320.3 %reduce-scatter.11.cloned.1.call-start = ((), (), s32[]{:S(2)}) async-start(), calls=%async_computation.14 | async-start | bytes 26738688 | tf_op jit(solution)/shard_map/reduce_scatter | solution.py:443
  495.2 515.4 %copy-start.66 = (f32[768]{0:T(1024)}, f32[768]{0:T(1024)S(1)}, u32[]{:S(2)}) copy-start(f32[768]{0:T(1024)S(1)} %convert_reduce_fusion.4) | copy-start | bytes 9220
  497.0 492.7 %copy-start.98 = (f32[768]{0:T(1024)}, f32[768]{0:T(1024)S(1)}, u32[]{:S(2)}) copy-start(f32[768]{0:T(1024)S(1)} %convert_reduce_fusion.3) | copy-start | bytes 9220
  979.7 30.9 copy-start.56
  981.2 29.5 copy-start.82
  1234.5 1316.8 %reduce-scatter.13.cloned.1.call-start = ((), (), s32[]{:S(2)}) async-start(), calls=%async_computation.15 | async-start | bytes 26738688 | tf_op jit(solution)/shard_map/reduce_scatter | solution.py:443
  1302.8 509.1 %copy-start.13 = (f32[512,768]{1,0:T(8,128)S(1)}, f32[512,768]{1,0:T(8,128)}, u32[]{:S(2)}) copy-start(f32[512,768]{1,0:T(8,128)} %copy-done.12) | copy-start | bytes 4718596
  1302.8 509.1 %copy-start.21 = (f32[512,768]{1,0:T(8,128)S(1)}, f32[512,768]{1,0:T(8,128)}, u32[]{:S(2)}) copy-start(f32[512,768]{1,0:T(8,128)} %copy-done.20) | copy-start | bytes 4718596
  1302.8 509.1 %copy-start.55 = (f32[512]{0:T(512)S(1)}, f32[512]{0:T(512)}, u32[]{:S(2)}) copy-start(f32[512]{0:T(512)} %copy-done.54) | copy-start | bytes 6148
  1302.8 509.1 %copy-start.65 = (f32[768]{0:T(1024)S(1)}, f32[768]{0:T(1024)}, u32[]{:S(2)}) copy-start(f32[768]{0:T(1024)} %copy-done.64) | copy-start | bytes 9220
  1302.8 509.1 %copy-start.79 = (f32[512]{0:T(512)S(1)}, f32[512]{0:T(512)}, u32[]{:S(2)}) copy-start(f32[512]{0:T(512)} %copy-done.78) | copy-start | bytes 6148
  1302.8 509.1 %copy-start.85 = (f32[512]{0:T(512)S(1)}, f32[512]{0:T(512)}, u32[]{:S(2)}) copy-start(f32[512]{0:T(512)} %copy-done.84) | copy-start | bytes 6148
  1307.8 509.9 %copy-start.61 = (f32[512]{0:T(512)S(1)}, f32[512]{0:T(512)}, u32[]{:S(2)}) copy-start(f32[512]{0:T(512)} %copy-done.60) | copy-start | bytes 6148
  2037.5 523.6 %reduce-scatter.21.cloned.1.call-start = ((), (), s32[]{:S(2)}) async-start(), calls=%async_computation.19 | async-start | bytes 1769472 | tf_op jit(solution)/shard_map/reduce_scatter | solution.py:480
  2041.5 536.2 %reduce-scatter.25.cloned.1.call-start = ((), (), s32[]{:S(2)}) async-start(), calls=%async_computation.21 | async-start | bytes 7077888 | tf_op jit(solution)/shard_map/reduce_scatter | solution.py:492
  2048.3 545.9 %reduce-scatter.29.cloned.1.call-start = ((), (), s32[]{:S(2)}) async-start(), calls=%async_computation.23 | async-start | bytes 7077888 | tf_op jit(solution)/shard_map/reduce_scatter | solution.py:498
  2056.2 550.1 %reduce-scatter.19.cloned.1.call-start = ((), (), s32[]{:S(2)}) async-start(), calls=%async_computation.18 | async-start | bytes 1769472 | tf_op jit(solution)/shard_map/reduce_scatter | solution.py:480
  2059.6 561.6 %reduce-scatter.17.cloned.1.call-start = ((), (), s32[]{:S(2)}) async-start(), calls=%async_computation.17 | async-start | bytes 5308416 | tf_op jit(solution)/shard_map/reduce_scatter | solution.py:474
  2065.1 572.7 %reduce-scatter.23.cloned.1.call-start = ((), (), s32[]{:S(2)}) async-start(), calls=%async_computation.20 | async-start | bytes 7077888 | tf_op jit(solution)/shard_map/reduce_scatter | solution.py:492
  2072.9 580.9 %reduce-scatter.27.cloned.1.call-start = ((), (), s32[]{:S(2)}) async-start(), calls=%async_computation.22 | async-start | bytes 7077888 | tf_op jit(solution)/shard_map/reduce_scatter | solution.py:498
  2080.8 588.0 %reduce-scatter.15.cloned.1.call-start = ((), (), s32[]{:S(2)}) async-start(), calls=%async_computation.16 | async-start | bytes 5308416 | tf_op jit(solution)/shard_map/reduce_scatter | solution.py:474
  2147.2 404.1 %copy-start.39 = (bf16[2,256,768]{2,1,0:T(8,128)(2,1)S(1)}, bf16[2,256,768]{2,1,0:T(8,128)(2,1)}, u32[]{:S(2)}) copy-start(bf16[2,256,768]{2,1,0:T(8,128)(2,1)} %copy-done.37) | copy-start | bytes 2359300
  2556.5 523.1 %all-reduce.21.cloned.1.call-start = ((), (), s32[]{:S(2)}) async-start(), calls=%async_computation.32 | async-start | bytes 28311552 | tf_op jit(solution)/shard_map/psum | solution.py:512
  2669.7 8.7 collective-permute-start.1
  2673.7 6.2 collective-permute-start
  2693.2 93.9 %collective-permute-start.2 = (bf16[10,768]{1,0:T(8,128)(2,1)S(1)}, bf16[10,768]{1,0:T(8,128)(2,1)S(1)}, u32[]{:S(2)}, u32[]{:S(2)}) collective-permute-start(bf16[10,768]{1,0:T(8,128)(2,1)S(1)} %get-tuple-element.1998), channel_id=1, source_target_pairs={{2,0},{4,2},{6,4},{8,6},{10,8},{12,10},{14,12},{16,14},{18,16},{20... | collective-permute-start | bytes 46088 | tf_op jit(solution)/shard_map/ppermute | solution.py:20
  2785.8 2.8 collective-permute-start.3
  (128 other events, 480.9 us)
Sparse Core Ops, SparseCore 0:
  11.5 15.3 all-gather.44
  32.4 153.1 all-gather.38
  189.0 150.1 all-gather.36
  340.7 7.4 all-gather.46
  350.1 15.5 all-gather.48
  367.1 15.6 all-gather.50
  384.3 13.8 all-gather.52
  489.1 212.3 all-gather.42
  704.2 150.1 all-gather.40
  856.4 7.4 all-gather.54
  866.0 15.5 all-gather.56
  883.6 15.6 all-gather.58
  1234.7 577.1 reduce-scatter.10
  2037.5 513.6 reduce-scatter.12
  2553.4 7.6 reduce-scatter.20
  2563.9 13.8 reduce-scatter.24
  2580.5 13.7 reduce-scatter.28
  2596.4 9.8 reduce-scatter.18
  2608.5 12.5 reduce-scatter.16
  2624.0 13.7 reduce-scatter.22
  2640.1 13.7 reduce-scatter.26
  2656.2 12.5 reduce-scatter.14
  2675.2 404.3 all-reduce.20
where the time goes:
time: 3040 us; the launch traced here: 3100 us
  waiting for transfers between devices  1820 us (60%)
  local copies, waits for them, and re-layouts  438 us (14%)
  matrix products  339 us (11%)
  other arithmetic  273 us (9%)
  blocking collectives  118 us (4%)
  loops' own time  89.3 us (3%)
    reduce_scatter x2, waiting for transfers between devices, backward_layer(): lax.psum_scatter(lax.map(one_piece, (keys_part, values_part, part_pos.res...  906 us
    psum x1, waiting for transfers between devices, backward_layer(): lax.psum(shards[0].astype(jnp.bfloat16), 'ctx').astype(jnp.float32)  290 us
    all_gather x2, waiting for transfers between devices, forward_layer(): lax.all_gather(mixed_rows[:, 2 * model_width:], 'ctx', axis=0, tiled=True)  275 us
    all_gather x2, waiting for transfers between devices, forward_layer(): lax.all_gather(mixed_rows[:, model_width:2 * model_width], 'ctx', axis=0,...  217 us
    unnamed x254, local copies, waits for them, and re-layouts  131 us
    dynamic_update_slice x64, local copies, waits for them, and re-layouts, backward_layer(): lax.map(one_piece, (keys_part, values_part, part_pos.reshape(pieces, piec...  95.5 us
    broadcast_in_dim x32, other arithmetic, backward_layer(): lax.map(one_piece, (keys_part, values_part, part_pos.reshape(pieces, piec...  89.4 us
    psum x1, blocking collectives, backward_layer(): lax.psum(shards[1].astype(jnp.bfloat16), 'ctx').astype(jnp.float32)  84.9 us
  transfers between devices with their start and end apart: 27, of which 18 were waited for; matrix products, arithmetic and copies ran while one was open for 18% of the time, Pallas kernels for 0%

commit v1 on v0

v1 whole, which is shorter than its diff:
```python
import functools

import jax
import jax.numpy as jnp
from jax import lax
from jax.experimental import pallas as pl
from jax.experimental.pallas import tpu as pltpu
from jax.sharding import PartitionSpec as P

MESH = pl.DeviceIdType.MESH
HEAD_DIM = 64
EPSILON = 1e-06
NEGATIVE = -1e30
DOC_MAX = 1024
inverse_root = 0.7071067811865476
inverse_tau = 0.3989422804014327
BF = jnp.bfloat16
F32 = jnp.float32
ANY = pl.BlockSpec(memory_space=pl.ANY)
WHOLE = pl.BlockSpec(memory_space=pltpu.VMEM)
VMEM_LIMIT = 58 << 20


def nn(a, b):
    return lax.dot_general(a, b, (((1,), (0,)), ((), ())), preferred_element_type=F32)


def nt(a, b):
    return lax.dot_general(a, b, (((1,), (1,)), ((), ())), preferred_element_type=F32)


def tn(a, b):
    return lax.dot_general(a, b, (((0,), (0,)), ((), ())), preferred_element_type=F32)


def full(shape):
    return pl.BlockSpec(shape, lambda j: (0,) * len(shape))


def shape_of(shape, dtype):
    return jax.ShapeDtypeStruct(shape, dtype)


def attn_fwd(a, w_in, bias, start_col, seg):
    rows, width = a.shape
    own = start_col.shape[0]
    back = rows - own
    quad = 4 * HEAD_DIM
    steps = width // quad
    blocks = own // seg

    def kernel(a_ref, wq, wk, wv, bq, bv, st_ref, q_ref, k_ref, v_ref, o_ref, l_ref):
        def project(i, carry):
            at = pl.ds(pl.multiple_of(i * seg, seg), seg)
            part = a_ref[at, :]
            k_ref[at, :] = nn(part, wk[...]).astype(BF)
            v_ref[at, :] = (nn(part, wv[...]) + bv[...]).astype(BF)
            return carry

        lax.fori_loop(0, rows // seg, project, 0)

        def project_q(i, carry):
            part = a_ref[pl.ds(pl.multiple_of(back + i * seg, seg), seg), :]
            got = (nn(part, wq[...]) + bq[...]).astype(BF)
            q_ref[pl.ds(pl.multiple_of(i * seg, seg), seg), :] = got * jnp.asarray(0.125, BF)
            return carry

        lax.fori_loop(0, blocks, project_q, 0)

        row = lax.broadcasted_iota(jnp.int32, (seg, seg), 0)
        col = lax.broadcasted_iota(jnp.int32, (seg, seg), 1)
        low = col <= row
        lane = lax.broadcasted_iota(jnp.int32, (seg, 2 * HEAD_DIM), 1)
        mid = back - seg
        col_mid = lax.broadcasted_iota(jnp.int32, (seg, mid), 1)

        def one_block(i, carry):
            base = pl.multiple_of(i * seg, seg)
            at = pl.ds(base, seg)
            st = st_ref[at, :] - base
            see_edge = jnp.where(low, col + back, col) >= st
            see_mid = (col_mid + seg) >= st
            logs = jnp.zeros((seg, 2 * HEAD_DIM), F32)
            for pair in range(2):
                lanes = slice(pair * 2 * HEAD_DIM, (pair + 1) * 2 * HEAD_DIM)
                qp = q_ref[at, lanes]
                k_far = k_ref[at, lanes]
                k_mid = k_ref[pl.ds(base + seg, mid), lanes]
                k_own = k_ref[pl.ds(base + back, seg), lanes]
                v_far = v_ref[at, lanes]
                v_mid = v_ref[pl.ds(base + seg, mid), lanes]
                v_own = v_ref[pl.ds(base + back, seg), lanes]
                outs = []
                for h in range(2):
                    mine = (lane >= HEAD_DIM) if h else (lane < HEAD_DIM)
                    qh = jnp.where(mine, qp, jnp.zeros_like(qp))
                    edge = jnp.where(low, nt(qh, k_own), nt(qh, k_far))
                    edge = jnp.where(see_edge, edge, NEGATIVE)
                    inner = jnp.where(see_mid, nt(qh, k_mid), NEGATIVE)
                    peak = jnp.maximum(
                        jnp.max(edge, axis=1, keepdims=True), jnp.max(inner, axis=1, keepdims=True)
                    )
                    edge = jnp.exp(edge - peak)
                    inner = jnp.exp(inner - peak)
                    total = jnp.sum(edge, axis=1, keepdims=True) + jnp.sum(inner, axis=1, keepdims=True)
                    got = nn(inner.astype(BF), v_mid)
                    got = got + nn(jnp.where(low, edge, 0.0).astype(BF), v_own)
                    got = got + nn(jnp.where(low, 0.0, edge).astype(BF), v_far)
                    outs.append(got / total)
                    logs = jnp.where(lane == 2 * pair + h, peak + jnp.log(total), logs)
                o_ref[at, lanes] = jnp.where(lane < HEAD_DIM, outs[0], outs[1]).astype(BF)
            l_ref[0, :, at] = logs.T[:8, :]
            return carry

        lax.fori_loop(0, blocks, one_block, 0)

    return pl.pallas_call(
        kernel,
        grid=(steps,),
        in_specs=[
            full((rows, width)),
            pl.BlockSpec((width, quad), lambda j: (0, j)),
            pl.BlockSpec((width, quad), lambda j: (0, steps + j)),
            pl.BlockSpec((width, quad), lambda j: (0, 2 * steps + j)),
            pl.BlockSpec((1, quad), lambda j: (0, j)),
            pl.BlockSpec((1, quad), lambda j: (0, steps + j)),
            full((own, 1)),
        ],
        out_specs=[
            pl.BlockSpec((own, quad), lambda j: (0, j)),
            pl.BlockSpec((rows, quad), lambda j: (0, j)),
            pl.BlockSpec((rows, quad), lambda j: (0, j)),
            pl.BlockSpec((own, quad), lambda j: (0, j)),
            pl.BlockSpec((1, 8, own), lambda j: (j, 0, 0)),
        ],
        out_shape=[
            shape_of((own, width), BF),
            shape_of((rows, width), BF),
            shape_of((rows, width), BF),
            shape_of((own, width), BF),
            shape_of((steps, 8, own), F32),
        ],
        compiler_params=pltpu.CompilerParams(vmem_limit_bytes=VMEM_LIMIT),
        name="attn_fwd",
    )(a, w_in, w_in, w_in, bias, bias, start_col)


def normalise(x):
    mean = jnp.mean(x, axis=-1, keepdims=True)
    centred = x - mean
    spread = jnp.mean(centred * centred, axis=-1, keepdims=True)
    scale = lax.rsqrt(spread + EPSILON)
    return centred * scale, scale


def ff_fwd(att, h, h_block, w_out, w_up, w_down, b_out, b_up, b_down, g1, s1, g2, s2):
    own, width = att.shape
    hidden = w_up.shape[1]
    chunk = 512
    steps = hidden // chunk

    def kernel(att_ref, h_ref, wo, wu, wd, bo, bu, bd, g1r, s1r, g2r, s2r,
               xh1, rs1, mid_low, act, gp, xh2, rs2, out, out_low, middle, acc):
        j = pl.program_id(0)

        @pl.when(j == 0)
        def _():
            x = h_ref[...].astype(F32) + (nn(att_ref[...], wo[...]) + bo[...])
            xh, sc = normalise(x)
            xh1[...] = xh
            rs1[...] = sc
            m = xh * g1r[...] + s1r[...]
            middle[...] = m
            mid_low[...] = m.astype(BF)
            acc[...] = jnp.zeros_like(acc)

        hid = nn(mid_low[...], wu[...]) + bu[...]
        scaled = hid * inverse_root
        half = 0.5 * (1.0 + lax.erf(scaled))
        low = (hid * half).astype(BF)
        act[...] = low
        gp[...] = (half + hid * (jnp.exp(-(scaled * scaled)) * inverse_tau)).astype(BF)
        acc[...] += nn(low, wd[...])

        @pl.when(j == steps - 1)
        def _():
            x = middle[...] + (acc[...] + bd[...])
            xh, sc = normalise(x)
            xh2[...] = xh
            rs2[...] = sc
            y = xh * g2r[...] + s2r[...]
            out[...] = y
            out_low[...] = y.astype(BF)

    row = full((1, width))
    return pl.pallas_call(
        kernel,
        grid=(steps,),
        in_specs=[
            full((own, width)),
            pl.BlockSpec((own, width), lambda j: (h_block, 0)),
            full((width, width)),
            pl.BlockSpec((width, chunk), lambda j: (0, j)),
            pl.BlockSpec((chunk, width), lambda j: (j, 0)),
            row,
            pl.BlockSpec((1, chunk), lambda j: (0, j)),
            row, row, row, row, row,
        ],
        out_specs=[
            full((own, width)),
            full((own, 1)),
            full((own, width)),
            pl.BlockSpec((own, chunk), lambda j: (0, j)),
            pl.BlockSpec((own, chunk), lambda j: (0, j)),
            full((own, width)),
            full((own, 1)),
            full((own, width)),
            full((own, width)),
        ],
        out_shape=[
            shape_of((own, width), F32),
            shape_of((own, 1), F32),
            shape_of((own, width), BF),
            shape_of((own, hidden), BF),
            shape_of((own, hidden), BF),
            shape_of((own, width), F32),
            shape_of((own, 1), F32),
            shape_of((own, width), F32),
            shape_of((own, width), BF),
        ],
        scratch_shapes=[pltpu.VMEM((own, width), F32), pltpu.VMEM((own, width), F32)],
        compiler_params=pltpu.CompilerParams(vmem_limit_bytes=VMEM_LIMIT),
        name="ff_fwd",
    )(att, h, w_out, w_up, w_down, b_out, b_up, b_down, g1, s1, g2, s2)


def norm_back(dy, xh, scale, gain):
    d = dy * gain
    mean_d = jnp.mean(d, axis=-1, keepdims=True)
    mean_dx = jnp.mean(d * xh, axis=-1, keepdims=True)
    return scale * (d - mean_d - xh * mean_dx)


def column_sum(x):
    return jnp.sum(x, axis=0, keepdims=True)


def ff_bwd(grads, xh2, rs2, g2, gp, act, w_down, w_up, mid_low, xh1, rs1, g1, w_out, att, pick):
    own, width = att.shape
    hidden = w_up.shape[1]
    chunk = width
    steps = hidden // chunk
    count = len(grads)
    groups = pick.shape[0]

    def kernel(*refs):
        g_refs = refs[:count]
        (xh2r, rs2r, g2r, gpr, actr, wd, wu, midr, xh1r, rs1r, g1r, wo, attr, pickr,
         dwd, dwu, dwo, small, dr1, do, delta, dr2, df, dm, mid_t) = refs[count:]
        j = pl.program_id(0)

        @pl.when(j == 0)
        def _():
            g = g_refs[0][...].astype(F32)
            for extra in g_refs[1:]:
                g = g + extra[...].astype(F32)
            xh = xh2r[...]
            small[...] = jnp.zeros_like(small)
            small[0:1, :] = column_sum(g * xh)
            small[1:2, :] = column_sum(g)
            d = norm_back(g, xh, rs2r[...], g2r[...])
            dr2[...] = d
            low = d.astype(BF)
            df[...] = low
            small[2:3, :] = column_sum(low.astype(F32))
            dm[...] = d
            mid_t[...] = midr[...].T

        dff = df[...]
        d_act = nt(dff, wd[...])
        dh = (d_act * gpr[...].astype(F32)).astype(BF)
        small[pl.ds(8 + j, 1), :] = column_sum(dh.astype(F32))
        dwd[...] = tn(actr[...], dff).astype(BF)
        dwu[...] = nn(mid_t[...], dh).astype(BF)
        dm[...] += nt(dh, wu[...])

        @pl.when(j == steps - 1)
        def _():
            g = dm[...]
            xh = xh1r[...]
            small[3:4, :] = column_sum(g * xh)
            small[4:5, :] = column_sum(g)
            d = norm_back(g, xh, rs1r[...], g1r[...])
            dr1[...] = d
            low = d.astype(BF)
            small[5:6, :] = column_sum(low.astype(F32))
            dwo[...] = tn(attr[...], low).astype(BF)
            back = nt(low, wo[...]).astype(BF)
            do[...] = back
            prod = back.astype(F32) * attr[...].astype(F32)
            high = prod.astype(BF)
            rest = (prod - high.astype(F32)).astype(BF)
            delta[...] = nt(pickr[...], high) + nt(pickr[...], rest)

    act_spec = pl.BlockSpec((own, chunk), lambda j: (0, j))
    return pl.pallas_call(
        kernel,
        grid=(steps,),
        in_specs=[full((own, width))] * count + [
            full((own, width)), full((own, 1)), full((1, width)),
            act_spec, act_spec,
            pl.BlockSpec((chunk, width), lambda j: (j, 0)),
            pl.BlockSpec((width, chunk), lambda j: (0, j)),
            full((own, width)), full((own, width)), full((own, 1)), full((1, width)),
            full((width, width)), full((own, width)), full((groups, width)),
        ],
        out_specs=[
            pl.BlockSpec((chunk, width), lambda j: (j, 0)),
            pl.BlockSpec((width, chunk), lambda j: (0, j)),
            full((width, width)),
            full((16, width)),
            full((own, width)),
            full((own, width)),
            full((groups, own)),
        ],
        out_shape=[
            shape_of((hidden, width), BF),
            shape_of((width, hidden), BF),
            shape_of((width, width), BF),
            shape_of((16, width), F32),
            shape_of((own, width), F32),
            shape_of((own, width), BF),
            shape_of((groups, own), F32),
        ],
        scratch_shapes=[
            pltpu.VMEM((own, width), F32),
            pltpu.VMEM((own, width), BF),
            pltpu.VMEM((own, width), F32),
            pltpu.VMEM((width, own), BF),
        ],
        compiler_params=pltpu.CompilerParams(vmem_limit_bytes=VMEM_LIMIT),
        name="ff_bwd",
    )(*grads, xh2, rs2, g2, gp, act, w_down, w_up, mid_low, xh1, rs1, g1, w_out, att, pick)


class Place:
    def __init__(self, contexts):
        self.n = contexts
        self.me = lax.axis_index("ctx")
        self.f = lax.axis_index("fsdp")
        self.odd = self.f % 2
        self.x = self.me % 2
        pair = self.me // 2
        self.is_low = self.x == self.odd
        self.chunk = jnp.where(self.is_low, pair, contexts - 1 - pair)
        self.half = jnp.where(self.is_low, 0, 1)
        self.mate = self.me + 1 - 2 * self.x

    def ctx_of(self, chunk):
        c = (chunk + self.n) % self.n
        return jnp.where(c < self.n // 2, 2 * c + self.odd, 2 * (self.n - 1 - c) + 1 - self.odd)


def greet(devices, count):
    barrier = pltpu.get_barrier_semaphore()
    for device in devices:
        pl.semaphore_signal(barrier, inc=1, device_id=device, device_id_type=MESH)
    pl.semaphore_wait(barrier, count)


def remote(src, dst, send, recv, device):
    return pltpu.make_async_remote_copy(
        src_ref=src, dst_ref=dst, send_sem=send, recv_sem=recv, device_id=device, device_id_type=MESH
    )


def gather_copies(shards, outs, bounce, peers, place, sems, loc):
    far, inward, outward = [], [], []
    for i, (src, dst) in enumerate(zip(shards, outs)):
        size = src.shape[0]
        here = dst.at[pl.ds(pl.multiple_of(place.f * size, 8), size)]
        for d, peer in enumerate(peers):
            far.append(remote(src, here, sems.at[0, i, d], sems.at[1, i, d], peer))
        inward.append(pltpu.make_async_copy(src, bounce[i], loc.at[0, i]))
        outward.append(pltpu.make_async_copy(bounce[i], here, loc.at[1, i]))
    return far, inward, outward


def fetch_window(x0, weights, small, contexts, fsdps, layer):
    seg, width = x0.shape[1:]
    own = 2 * seg
    rows = 3 * own
    count = len(weights)

    def kernel(*refs):
        x_ref, w_refs, small_ref = refs[0], refs[1:1 + count], refs[1 + count]
        win, w_outs, small_out = refs[2 + count], refs[3 + count:3 + 2 * count], refs[3 + 2 * count]
        send, recv, w_sem, w_loc, s_sem, loc = refs[4 + 2 * count:10 + 2 * count]
        bounce = refs[10 + 2 * count:]
        p = Place(contexts)
        peers = [(p.me, (p.f + d) % fsdps) for d in range(1, fsdps)]
        mate = (p.mate, p.f)
        ahead = [(p.ctx_of(p.chunk + s), p.f) for s in (1, 2)]
        behind = [(p.ctx_of(p.chunk - s), p.f) for s in (1, 2)]
        greet([mate] + behind + peers, 3 + fsdps - 1)
        slot = p.odd
        other = 1 - slot
        mine = x_ref.at[p.half]

        def at(start, s):
            return win.at[pl.ds(pl.multiple_of(start + s * seg, seg), seg)]

        swap = remote(x_ref.at[1 - p.half], at(2 * own, other), send.at[0], recv.at[0], mate)
        swap.start()
        keep = pltpu.make_async_copy(mine, at(2 * own, slot), loc.at[0])
        keep.start()
        first = [
            remote(mine, at((2 - s) * own, slot), send.at[s], recv.at[s], ahead[s - 1]) for s in (1, 2)
        ]
        for copy in first:
            copy.start()
        gathers, inward, outward = gather_copies(
            [r.at[layer] for r in w_refs], w_outs, bounce, peers, p, w_sem, w_loc
        )
        for i, peer in enumerate(peers):
            gathers.append(remote(small_ref, small_out.at[p.f], s_sem.at[0, i], s_sem.at[1, i], peer))
        gathers.append(pltpu.make_async_copy(small_ref, small_out.at[p.f], loc.at[1]))
        for copy in gathers + inward:
            copy.start()
        for copy, follow in zip(inward, outward):
            copy.wait()
            follow.start()
        swap.wait_recv()
        second = [
            remote(at(2 * own, other), at((2 - s) * own, other), send.at[2 + s], recv.at[2 + s], ahead[s - 1])
            for s in (1, 2)
        ]
        for copy in second:
            copy.start()
        keep.wait()
        for copy in gathers + outward + first + second:
            copy.wait()
        swap.wait_send()

    full_weights = [
        shape_of((w.shape[1] * fsdps,) + w.shape[2:], w.dtype) for w in weights
    ]
    return pl.pallas_call(
        kernel,
        out_shape=[shape_of((rows, width), BF)] + full_weights
        + [shape_of((fsdps,) + small.shape, small.dtype)],
        in_specs=[WHOLE] + [ANY] * count + [WHOLE],
        out_specs=[ANY] * (2 + count),
        scratch_shapes=[
            pltpu.SemaphoreType.DMA((5,)),
            pltpu.SemaphoreType.DMA((5,)),
            pltpu.SemaphoreType.DMA((2, count, max(1, fsdps - 1))),
            pltpu.SemaphoreType.DMA((2, count)),
            pltpu.SemaphoreType.DMA((2, max(1, fsdps - 1))),
            pltpu.SemaphoreType.DMA((2,)),
        ] + [pltpu.VMEM(w.shape[1:], w.dtype) for w in weights],
        compiler_params=pltpu.CompilerParams(
            collective_id=0, has_side_effects=True, vmem_limit_bytes=VMEM_LIMIT
        ),
        name="fetch_window",
    )(x0, *weights, small)


def share_window(low, weights, cot, contexts, fsdps, layer):
    own, width = low.shape
    seg = own // 2
    rows = 3 * own
    count = len(weights)

    def kernel(*refs):
        x_ref, w_refs, cot_ref = refs[0], refs[1:1 + count], refs[1 + count]
        win, w_outs, cot_out = refs[2 + count], refs[3 + count:3 + 2 * count], refs[3 + 2 * count]
        send, recv, w_sem, w_loc, loc = refs[4 + 2 * count:9 + 2 * count]
        bounce = refs[9 + 2 * count:]
        p = Place(contexts)
        peers = [(p.me, (p.f + d) % fsdps) for d in range(1, fsdps)]
        mate = (p.mate, p.f)
        ahead = [(p.ctx_of(p.chunk + s), p.f) for s in (1, 2)]
        behind = [(p.ctx_of(p.chunk - s), p.f) for s in (1, 2)]
        greet([mate] + behind + peers, 3 + fsdps - 1)
        slot = p.odd

        def part(s):
            return cot_out.at[pl.ds(pl.multiple_of(s * seg, seg), seg)]

        halo = [
            remote(x_ref, win.at[pl.ds((2 - s) * own, own)], send.at[s], recv.at[s], ahead[s - 1])
            for s in (1, 2)
        ]
        swap = remote(cot_ref.at[1 - p.half], part(1 - slot), send.at[0], recv.at[0], mate)
        keep = pltpu.make_async_copy(cot_ref.at[p.half], part(slot), loc.at[0])
        copy_own = pltpu.make_async_copy(x_ref, win.at[pl.ds(2 * own, own)], loc.at[1])
        copies = halo + [swap, keep, copy_own]
        far, inward, outward = gather_copies(
            [r.at[layer] for r in w_refs], w_outs, bounce, peers, p, w_sem, w_loc
        )
        for copy in copies + far + inward:
            copy.start()
        for copy, follow in zip(inward, outward):
            copy.wait()
            follow.start()
        for copy in copies + far + outward:
            copy.wait()

    full_weights = [
        shape_of((w.shape[1] * fsdps,) + w.shape[2:], w.dtype) for w in weights
    ]
    return pl.pallas_call(
        kernel,
        out_shape=[shape_of((rows, width), BF)] + full_weights + [shape_of((own, width), BF)],
        in_specs=[WHOLE] + [ANY] * count + [WHOLE],
        out_specs=[ANY] * (2 + count),
        scratch_shapes=[
            pltpu.SemaphoreType.DMA((3,)),
            pltpu.SemaphoreType.DMA((3,)),
            pltpu.SemaphoreType.DMA((2, count, max(1, fsdps - 1))),
            pltpu.SemaphoreType.DMA((2, count)),
            pltpu.SemaphoreType.DMA((2,)),
        ] + [pltpu.VMEM(w.shape[1:], w.dtype) for w in weights],
        compiler_params=pltpu.CompilerParams(
            collective_id=1, has_side_effects=True, vmem_limit_bytes=VMEM_LIMIT
        ),
        name="share_window",
    )(low, *weights, cot)


class Piece:
    def __init__(self, sums, u, r, ready=False):
        pattern = sums.ready_pattern if ready else sums.pattern
        self.k = 5 * u + r
        self.slot = self.k + sums.n if ready else self.k
        self.ready = ready
        self.deep = is_deep(pattern[r])
        same = [is_deep(kind) == self.deep for kind in pattern]
        self.i = u * sum(same) + sum(same[:r])
        x_first = pattern[r] in ("xyz", "zxy")
        b0, b1 = (sums.bx, sums.by) if x_first else (sums.by, sums.bx)
        self.p0, self.p1 = (sums.x, sums.y) if x_first else (sums.y, sums.x)
        rows = sums.rows
        size = rows // 4 if self.deep else rows // 2
        base = sums.m * (rows // 2) if self.deep else 0
        self.first = (base + b0 * size, size)
        self.given = (base + (1 - b0) * size, size)
        start = base + b0 * size
        self.second = (start + b1 * (size // 2), size // 2)
        self.given_1 = (start + (1 - b1) * (size // 2), size // 2)
        self.column = (0, rows) if self.deep else self.second
        start, size = self.column
        self.mine = (start + sums.m * (size // 2), size // 2)
        self.theirs = (start + (1 - sums.m) * (size // 2), size // 2)
        self.own = self.second if self.deep else self.mine


def is_deep(kind):
    return kind[0] == "z"


FLAT = ("xyz", "yxz", "xyz", "yxz", "zxy")
MIXED = ("xyz", "zyx", "yxz", "zyx", "xyz")


class Sums:
    height = 128

    def __init__(self, shard, count, contexts, fsdps, width, gather=True, early=None, late_round=0, ready=0, lag=4, pattern=MIXED,
                 ready_pattern=FLAT):
        if contexts != 16:
            raise ValueError("needs 16 contexts")
        self.valid = min(shard, self.height)
        self.n = count
        self.rows = self.height
        self.width = width
        self.fsdps = fsdps
        self.others = fsdps - 1
        self.stride = contexts // 4
        self.gather = gather
        self.early = count if early is None else early
        self.gap = 0 if early is None else max(0, late_round - self.early // 5)
        self.ready = ready
        self.pattern, self.ready_pattern = pattern, ready_pattern
        self.lag = lag
        self.stages = 9 if gather else 5
        last = max(count + 5 * self.gap + (self.stages - 1) * self.lag, ready + 4 * self.lag if ready else 0)
        self.rounds = -(-last // 5)

    def scratch(self):
        n, r, w = self.n, self.rows, self.width
        nd = max(1, self.others)
        n_c = sum(is_deep(self.pattern[k % 5]) for k in range(n))
        n_a = max(1, n - n_c)
        n_c = max(1, n_c)
        dma = pltpu.SemaphoreType.DMA
        both = n + self.ready
        return [
            pltpu.VMEM((n, r, w), BF),
            pltpu.VMEM((n, nd, self.valid, w), BF),
            pltpu.VMEM((n_a, r // 2, w), BF),
            pltpu.VMEM((n_a, r // 4, w), BF),
            pltpu.VMEM((n_a, r // 4, w), BF),
            pltpu.VMEM((n_a, r // 8, w), BF),
            pltpu.VMEM((n_c, r // 4, w), BF),
            pltpu.VMEM((n_c, r // 8, w), BF),
            pltpu.VMEM((n_c, r, w), BF),
            pltpu.VMEM((n_c, r // 2, w), BF),
            dma((n,)), dma((nd,)), dma((n, nd)),
            dma((4, 2)), dma((4, n)),
            dma((10, 2)), dma((5, both)), dma((both,)),
        ]

    def bind(self, refs, out, compact=None, ready_in=None, ready_out=None):
        self.acc, self.got_f = refs[0], refs[1]
        self.got_0, self.got_1 = (refs[2], refs[6]), (refs[3], refs[7])
        self.got_z, self.got_y = (refs[4], refs[8]), (refs[5], refs[9])
        self.s_loc, self.s_f, self.r_f, self.send, self.recv, self.g_send, self.g_recv, self.s_own = refs[10:18]
        self.out, self.compact, self.ready_in, self.ready_out = out, compact, ready_in, ready_out
        me, f = lax.axis_index("ctx"), lax.axis_index("fsdp")
        self.me, self.f = me, f
        self.bx, self.by, z = me % 2, me // 2 % 2, me // self.stride
        self.mid = (z == 1) | (z == 2)
        self.end = (z == 0) | (z == 3)
        self.m = jnp.where(z == 2, 1, 0)
        up, down = me + self.stride, me - self.stride
        self.x = (me + 1 - 2 * self.bx, f)
        self.y = (me + 2 - 4 * self.by, f)
        self.to_mid = (jnp.where(z == 0, up, down), f)
        self.other_mid = (jnp.where(z == 1, up, down), f)
        self.to_end = (jnp.where(z == 1, down, up), f)
        self.peers = [(me, (f + d) % self.fsdps) for d in range(1, self.fsdps)]
        if self.rows > self.valid:
            self.acc[:, self.valid:, :] = jnp.zeros((self.n, self.rows - self.valid, self.width), BF)

    def signal_neighbours(self, barrier):
        def tell(device):
            pl.semaphore_signal(barrier, inc=1, device_id=device, device_id_type=MESH)

        for device in self.peers + [self.x, self.y]:
            tell(device)

        @pl.when(self.end)
        def _():
            tell(self.to_mid)

        @pl.when(self.mid)
        def _():
            tell(self.other_mid)
            tell(self.to_end)

        return self.others + 2 + jnp.where(self.mid, 2, 1)

    def load(self, i, source):
        pltpu.make_async_copy(source(self.f), self.acc.at[i, pl.ds(0, self.valid)], self.s_loc.at[i]).start()
        for d, peer in enumerate(self.peers):
            remote(source(peer[1]), self.got_f.at[i, d], self.s_f.at[d], self.r_f.at[i, d], peer).start()

    def f_copy(self, k, d):
        ref = self.got_f.at[k, d]
        return remote(ref, ref, self.s_f.at[d], self.r_f.at[k, d], self.peers[d])

    def at(self, p, where):
        return self.acc.at[p.k, pl.ds(pl.multiple_of(where[0], 16), where[1])]

    def make(self, slot, p, src, dst, device):
        return remote(src, dst, self.send.at[slot, int(p.deep)], self.recv.at[slot, p.k], device)

    def copy_0(self, p):
        return self.make(0, p, self.at(p, p.given), self.got_0[p.deep].at[p.i], p.p0)

    def copy_1(self, p):
        return self.make(1, p, self.at(p, p.given_1), self.got_1[p.deep].at[p.i], p.p1)

    def copy_z(self, p):
        return self.make(2, p, self.at(p, p.column), self.got_z[p.deep].at[p.i], self.to_mid)

    def copy_y(self, p):
        return self.make(3, p, self.at(p, p.theirs), self.got_y[p.deep].at[p.i], self.other_mid)

    def add(self, p, where, part):
        rows = pl.ds(pl.multiple_of(where[0], 16), where[1])
        self.acc[p.k, rows, :] = self.acc[p.k, rows, :] + part[...]

    def take_f(self, p):
        mine = self.acc.at[p.k, pl.ds(0, self.valid)]
        pltpu.make_async_copy(mine, mine, self.s_loc.at[p.k]).wait()
        for d in range(self.others):
            self.f_copy(p.k, d).wait_recv()
        if self.others == 1:
            self.add(p, (0, self.valid), self.got_f.at[p.k, 0])
        else:
            value = mine[...].astype(F32)
            for d in range(self.others):
                value = value + self.got_f[p.k, d].astype(F32)
            mine[...] = value.astype(BF)

    def take_0(self, p):
        self.copy_0(p).wait_recv()
        self.add(p, p.first, self.got_0[p.deep].at[p.i])

    def take_1(self, p):
        self.copy_1(p).wait_recv()
        self.add(p, p.second, self.got_1[p.deep].at[p.i])

    def send_z(self, p):
        @pl.when(self.end)
        def _():
            self.copy_z(p).start()

    def take_z(self, p):
        @pl.when(self.mid)
        def _():
            self.copy_z(p).wait_recv()
            self.add(p, p.column, self.got_z[p.deep].at[p.i])
            self.copy_y(p).start()

    def take_y(self, p):
        self.copy_y(p).wait_recv()
        self.add(p, p.mine, self.got_y[p.deep].at[p.i])

    def place(self, p, where):
        ref = self.ready_out if p.ready else self.out
        return ref.at[p.k, pl.ds(pl.multiple_of(where[0], 16), where[1])]

    def held(self, p):
        return self.ready_in.at[p.k] if p.ready else self.at(p, p.own)

    def send_to(self, slot, p, where, device, held=False):
        spot = self.place(p, where)
        src = self.held(p) if held else spot
        sent = self.g_send.at[slot + 5 * p.ready, int(p.deep)]
        return remote(src, spot, sent, self.g_recv.at[slot, p.slot], device)

    def save(self, p):
        return pltpu.make_async_copy(self.held(p), self.place(p, p.own), self.s_own.at[p.slot])

    def gm(self, p):
        return self.send_to(0, p, p.mine, self.other_mid, held=not p.deep)

    def ge(self, p):
        return self.send_to(1, p, p.mine, self.to_end, held=not p.deep)

    def gf(self, p):
        return self.send_to(2, p, p.theirs, self.to_end)

    def g1(self, p):
        return self.send_to(3, p, p.second, p.p1, held=p.deep)

    def g0(self, p):
        return self.send_to(4, p, p.first, p.p0)

    def gather_stage(self, s, p):
        def on_mid(f):
            pl.when(self.mid)(f)

        def on_end(f):
            pl.when(self.end)(f)

        if not p.deep:
            if s == 0:
                @on_mid
                def _():
                    self.save(p).start()
                    self.gm(p).start()
                    self.ge(p).start()
            elif s == 1:
                @on_mid
                def _():
                    self.gm(p).wait_recv()
                    self.gf(p).start()
            elif s == 2:
                @on_mid
                def _():
                    self.save(p).wait()

                @on_end
                def _():
                    self.ge(p).wait_recv()
                    self.gf(p).wait_recv()

                self.g1(p).start()
            elif s == 3:
                self.g1(p).wait_recv()
                self.g0(p).start()
            else:
                self.g0(p).wait_recv()
            return
        if s == 4:
            @on_end
            def _():
                self.ge(p).wait_recv()
                self.gf(p).wait_recv()
            return

        @on_mid
        def _():
            if s == 0:
                self.save(p).start()
                self.g1(p).start()
            elif s == 1:
                self.save(p).wait()
                self.g1(p).wait_recv()
                self.g0(p).start()
            elif s == 2:
                self.g0(p).wait_recv()
                self.gm(p).start()
                self.ge(p).start()
            else:
                self.gm(p).wait_recv()
                self.gf(p).start()

    def scatter_stage(self, s, p):
        if s == 0:
            self.take_f(p)
            if p.deep:
                self.send_z(p)
            else:
                self.copy_0(p).start()
        elif not p.deep:
            if s == 1:
                self.take_0(p)
                self.copy_1(p).start()
            elif s == 2:
                self.take_1(p)
                self.send_z(p)
            elif s == 3:
                self.take_z(p)
            else:
                @pl.when(self.mid)
                def _():
                    self.take_y(p)
        elif s == 1:
            self.take_z(p)
        else:
            @pl.when(self.mid)
            def _():
                if s == 2:
                    self.take_y(p)
                    self.copy_0(p).start()
                elif s == 3:
                    self.take_0(p)
                    self.copy_1(p).start()
                else:
                    self.take_1(p)

        if s == 4 and not self.gather:
            @pl.when(self.mid)
            def _():
                self.compact[p.k] = self.at(p, p.own)[...]

    def round(self, t):
        for j in range(5):
            for s in reversed(range(self.stages)):
                q, r = divmod(j - s * self.lag, 5)
                u = t + q
                at = 5 * u + r
                if self.gap:
                    late = at >= self.early + 5 * self.gap
                    live = (at >= 0) & (late | (at < self.early)) & (at < self.n + 5 * self.gap)
                    u = jnp.where(late, u - self.gap, u)
                else:
                    live = (at >= 0) & (at < self.n)

                @pl.when(live)
                def _(s=s, u=u, r=r):
                    p = Piece(self, u, r)
                    if s < 5:
                        self.scatter_stage(s, p)
                    if s >= 4 and self.gather:
                        self.gather_stage(s - 4, p)

            for s in reversed(range(5 if self.ready else 0)):
                q, r = divmod(j - s * self.lag, 5)
                u = t + q
                at = 5 * u + r

                @pl.when((at >= 0) & (at < self.ready))
                def _(s=s, u=u, r=r):
                    self.gather_stage(s, Piece(self, u, r, True))

    def finish(self):
        def drained(sem, height, pattern, count, deep):
            pieces = sum(is_deep(pattern[k % 5]) == deep for k in range(count))
            while pieces:
                some = min(pieces, self.n * self.rows // height)
                whole, rest = divmod(some * height, self.rows)
                if whole:
                    ref = self.acc.at[pl.ds(0, whole)]
                    pltpu.make_async_copy(ref, ref, sem).wait()
                if rest:
                    ref = self.acc.at[0, pl.ds(0, rest)]
                    pltpu.make_async_copy(ref, ref, sem).wait()
                pieces -= some

        for d in range(self.others):
            ref = self.got_f.at[:, d]
            pltpu.make_async_copy(ref, ref, self.s_f.at[d]).wait()
        rows = self.rows
        for deep in (False, True):
            i = int(deep)
            size = rows // 4 if deep else rows // 2
            column = rows if deep else rows // 4
            for count, ready in ((self.n, False), (self.ready, True)):
                pattern = self.ready_pattern if ready else self.pattern
                across, along_end, along_mid = [], [], []
                if not ready:
                    across += [(self.send.at[0, i], size), (self.send.at[1, i], size // 2)]
                    along_end += [(self.send.at[2, i], column)]
                    along_mid += [(self.send.at[3, i], column // 2)]
                if ready or self.gather:
                    base = 5 * ready
                    across += [(self.g_send.at[base + 3, i], size // 2), (self.g_send.at[base + 4, i], size)]
                    along_mid += [(self.g_send.at[base + j, i], column // 2) for j in range(3)]

                def wait(copies, pattern=pattern, count=count, deep=deep):
                    for sem, height in copies:
                        drained(sem, height, pattern, count, deep)

                if deep:
                    along_mid = across + along_mid
                else:
                    wait(across)

                @pl.when(self.mid)
                def _(along_mid=along_mid, wait=wait):
                    wait(along_mid)

                if along_end:
                    @pl.when(self.end)
                    def _(along_end=along_end, wait=wait):
                        wait(along_end)


def piece_list(arrays, width, fsdps, height):
    shard = width // fsdps
    size = min(shard, height)
    found = []
    for i, shape in enumerate(arrays):
        r, c = shape[-2:]
        per = r // fsdps
        for at in range(shape[0]) if len(shape) == 3 else [None]:
            for lane in range(c // width):
                for sub in range(per // size):
                    found.append((i, at, per, sub * size, lane * width))
    return found


STRIDE, STRIDE_LAST = 2, 3


def attn_bwd(a, w_in, q, k, v, do, logs, delta, start_row, dr1, seg, contexts, fsdps, early, extra, ready=None):
    rows, width = a.shape
    own = q.shape[0]
    back = rows - own
    if rows != 2 * width:
        raise ValueError("window rows")
    pair_lanes = 2 * HEAD_DIM
    pairs = width // pair_lanes
    last = len(extra) > 1
    shard = width // fsdps
    pieces = piece_list([g.shape for g in early], width, fsdps, Sums.height)
    n_early = len(pieces)
    size = min(shard, Sums.height)
    n_late = 3 * (shard // size) + 1 if last else 0
    blocks = own // seg
    cut = 256
    t_back = blocks * pairs
    t_own = t_back + back // seg
    t_weight = t_own + own // seg
    t_rest = t_weight + width // cut
    n_ready = ready.shape[0] if last else 0
    stride = STRIDE_LAST if last else STRIDE
    late_round = max(t_rest // stride + 1, -(-n_early // 5))
    engine = Sums(
        shard, n_early + n_late, contexts, fsdps, width, gather=last, early=n_early if last else None,
        late_round=late_round, ready=n_ready, lag=4 if last else 6, pattern=MIXED if last else FLAT,
    )
    rounds = t_rest + max(engine.rounds - t_rest // stride, 9)
    n_x, n_e = len(extra), len(early)

    def kernel(*refs):
        (a_hbm, w_hbm, q_ref, k_ref, v_ref, do_ref, l_ref, d_ref, st_ref, dr1_hbm) = refs[:10]
        x_refs, e_refs = refs[10:10 + n_x], refs[10 + n_x:10 + n_x + n_e]
        rest = refs[10 + n_x + n_e:]
        if last:
            ready_in, out_sums, dealt, memory, ready_out = rest[:5]
            rest = rest[5:]
        else:
            out_sums, dealt, memory, g_own, one, two, dw_out, db_out = rest[:8]
            rest = rest[8:]
        (w_ref, dk, dv, dk_all, dv_all, dq_all, g_back, dw, send, recv, loc, m_send, m_recv) = rest[:13]
        rest = rest[13:]
        if last:
            g_own, one, two, sm, sm_low = rest[:5]
            rest = rest[5:]
            low_ref = one
        else:
            low_ref = x_refs[0]
        if last:
            engine.bind(rest, out_sums, ready_in=ready_in, ready_out=ready_out)
        else:
            engine.bind(rest, None, compact=out_sums)
        p = Place(contexts)
        mate = (p.mate, p.f)
        ahead = [(p.ctx_of(p.chunk + s), p.f) for s in (1, 2)]
        behind = [(p.ctx_of(p.chunk - s), p.f) for s in (1, 2)]
        slot = p.odd
        shift = -1 if last else 1

        def holder(block):
            b = (block + 2 * contexts) % (2 * contexts)
            return jnp.where(b < contexts, b, 2 * contexts - 1 - b), jnp.where(b < contexts, 0, 1)

        targets = [holder(2 * p.chunk + s + shift) for s in (0, 1)]
        sources = [
            p.ctx_of(((b - shift + 2 * contexts) % (2 * contexts)) // 2)
            for b in (p.me, 2 * contexts - 1 - p.me)
        ]

        barrier = pltpu.get_barrier_semaphore()
        for device in [mate] + ahead:
            pl.semaphore_signal(barrier, inc=1, device_id=device, device_id_type=MESH)
        for ctx in sources:
            @pl.when(ctx != p.me)
            def _(ctx=ctx):
                pl.semaphore_signal(barrier, inc=1, device_id=(ctx, p.f), device_id_type=MESH)
        count = 3 + engine.signal_neighbours(barrier)
        for ctx, _ in targets:
            count = count + jnp.where(ctx != p.me, 1, 0)
        pl.semaphore_wait(barrier, count)

        fetch_w = pltpu.make_async_copy(w_hbm, w_ref, loc.at[1])
        fetch_r = pltpu.make_async_copy(dr1_hbm, g_own, loc.at[4])
        fetch_w.start()
        fetch_r.start()
        for i, (e, at, per, sub, lane) in enumerate(pieces):
            def source(part, e=e, at=at, per=per, sub=sub, lane=lane):
                rows_at = pl.ds(pl.multiple_of(part * per + sub, 8), size)
                ref = e_refs[e] if at is None else e_refs[e].at[at]
                return ref.at[rows_at, pl.ds(lane, width)]

            engine.load(i, source)

        def block_rows(s):
            return pl.ds(pl.multiple_of(s * seg, seg), seg)

        def deal(start):
            there = remote(low_ref.at[block_rows(1 - slot)], dealt.at[p.half], send.at[0], recv.at[0], mate)
            here = pltpu.make_async_copy(low_ref.at[block_rows(slot)], dealt.at[p.half], loc.at[2])
            if start:
                there.start()
                here.start()
            else:
                there.wait()
                here.wait()

        def memory_copies(start):
            for s, (ctx, half) in enumerate(targets):
                first = s * seg + (seg - 16 if shift > 0 else 0)
                src, dst = low_ref.at[pl.ds(first, 16)], memory.at[half]
                away = remote(src, dst, m_send.at[s], m_recv.at[half], (ctx, p.f))

                @pl.when(ctx != p.me)
                def _(away=away):
                    if start:
                        away.start()
                    else:
                        away.wait_send()

                if start:
                    @pl.when(ctx == p.me)
                    def _(src=src, dst=dst, half=half):
                        pltpu.make_async_copy(src, dst, m_recv.at[half]).start()

            if not start:
                for half in range(2):
                    pltpu.make_async_copy(memory.at[half], memory.at[half], m_recv.at[half]).wait()

        if not last:
            deal(True)
            memory_copies(True)

        key = lax.broadcasted_iota(jnp.int32, (seg, seg), 0)
        qry = lax.broadcasted_iota(jnp.int32, (seg, seg), 1)
        low = key <= qry
        lane_id = lax.broadcasted_iota(jnp.int32, (seg, pair_lanes), 1)
        mid = back - seg
        key_mid = lax.broadcasted_iota(jnp.int32, (mid, seg), 0)

        def one_block(index):
            pair, i = index // blocks, index % blocks
            lanes = pl.ds(pl.multiple_of(pair * pair_lanes, pair_lanes), pair_lanes)

            @pl.when(i == 0)
            def _():
                dk[...] = jnp.zeros_like(dk)
                dv[...] = jnp.zeros_like(dv)

            base = pl.multiple_of(i * seg, seg)
            at = pl.ds(base, seg)
            st = st_ref[:, at] - base
            see_edge = jnp.where(low, key + back, key) >= st
            see_mid = (key_mid + seg) >= st
            far, near, inn = at, pl.ds(base + back, seg), pl.ds(base + seg, mid)
            qp, dop = q_ref[at, lanes], do_ref[at, lanes]
            k_far, k_mid, k_own = k_ref[far, lanes], k_ref[inn, lanes], k_ref[near, lanes]
            k_far_t, k_mid_t, k_own_t = k_far.T, k_mid.T, k_own.T
            v_far, v_mid, v_own = v_ref[far, lanes], v_ref[inn, lanes], v_ref[near, lanes]
            q2, do2, p_far, p_mid, p_own, s_far, s_mid, s_own, dqs = [], [], [], [], [], [], [], [], []
            for h in range(2):
                mine = (lane_id >= HEAD_DIM) if h else (lane_id < HEAD_DIM)
                qh = jnp.where(mine, qp, jnp.zeros_like(qp))
                doh = jnp.where(mine, dop, jnp.zeros_like(dop))
                stat = pair % 2 * 2 + h
                log_row = l_ref[pair // 2, pl.ds(stat, 1), at]
                del_row = d_ref[pair // 2, pl.ds(stat, 1), at]
                edge = jnp.where(low, nt(k_own, qh), nt(k_far, qh))
                edge = jnp.exp(jnp.where(see_edge, edge - log_row, NEGATIVE))
                inner = jnp.exp(jnp.where(see_mid, nt(k_mid, qh) - log_row, NEGATIVE))
                d_edge = edge * (jnp.where(low, nt(v_own, doh), nt(v_far, doh)) - del_row)
                d_inner = (inner * (nt(v_mid, doh) - del_row)).astype(BF)
                d_own = jnp.where(low, d_edge, 0.0).astype(BF)
                d_far = jnp.where(low, 0.0, d_edge).astype(BF)
                part = slice(h * HEAD_DIM, (h + 1) * HEAD_DIM)
                dqs.append(nn(k_mid_t[part], d_inner) + nn(k_own_t[part], d_own) + nn(k_far_t[part], d_far))
                q2.append(qh)
                do2.append(doh)
                p_far.append(jnp.where(low, 0.0, edge).astype(BF))
                p_own.append(jnp.where(low, edge, 0.0).astype(BF))
                p_mid.append(inner.astype(BF))
                s_far.append(d_far)
                s_own.append(d_own)
                s_mid.append(d_inner)
            q2 = jnp.concatenate(q2, axis=0)
            do2 = jnp.concatenate(do2, axis=0)
            dv[far, :] += nn(jnp.concatenate(p_far, axis=1), do2)
            dv[inn, :] += nn(jnp.concatenate(p_mid, axis=1), do2)
            dv[near, :] += nn(jnp.concatenate(p_own, axis=1), do2)
            dk[far, :] += nn(jnp.concatenate(s_far, axis=1), q2)
            dk[inn, :] += nn(jnp.concatenate(s_mid, axis=1), q2)
            dk[near, :] += nn(jnp.concatenate(s_own, axis=1), q2)
            dq_all[at, lanes] = (jnp.concatenate(dqs, axis=0).T * 0.125).astype(BF)

            @pl.when(i == blocks - 1)
            def _():
                dk_all[:, lanes] = dk[...].astype(BF)
                dv_all[:, lanes] = dv[...].astype(BF)

        bufs = (one, two)

        def back_rows(i):
            at = block_rows(i)
            got = nt(dk_all[at, :], w_ref[:, width:2 * width]) + nt(dv_all[at, :], w_ref[:, 2 * width:])
            g_back[at, :] = got.astype(BF)

        order = (1 - slot, slot)

        def halo_copies():
            found = []
            for i, s in enumerate(order):
                for j in (1, 2):
                    at = pl.multiple_of((2 - j) * own + s * seg, seg)
                    found.append(
                        remote(
                            g_back.at[pl.ds(at, seg)], bufs[j - 1].at[block_rows(s)],
                            send.at[2 * i + j], recv.at[2 * i + j], behind[j - 1],
                        )
                    )
            return found

        def own_rows(i):
            at = block_rows(i)
            there = pl.ds(pl.multiple_of(back + i * seg, seg), seg)
            got = nt(dk_all[there, :], w_ref[:, width:2 * width]) + nt(dv_all[there, :], w_ref[:, 2 * width:])
            g_own[at, :] += got + nt(dq_all[at, :], w_ref[:, :width])

        fetch_a = [
            pltpu.make_async_copy(
                a_hbm.at[pl.ds(i * width, width)], w_ref.at[:, pl.ds(i * width, width)], loc.at[i]
            )
            for i in range(2)
        ]

        def weight_rows(i):
            start = pl.multiple_of(i * cut, cut)
            at = pl.ds(start, cut)
            first = w_ref[:, at].T
            second = w_ref[:, pl.ds(pl.multiple_of(width + start, cut), cut)].T
            dw[0, at, :] = nn(second[:, back - width:], dq_all[...]).astype(BF)
            dw[1, at, :] = (nn(first, dk_all[:width, :]) + nn(second, dk_all[width:, :])).astype(BF)
            dw[2, at, :] = (nn(first, dv_all[:width, :]) + nn(second, dv_all[width:, :])).astype(BF)

        def late_pieces():
            for j in range(3):
                for sub in range(shard // size):
                    engine.load(
                        n_early + j * (shard // size) + sub,
                        lambda part, j=j, sub=sub: dw.at[j, pl.ds(pl.multiple_of(part * shard + sub * size, 16), size)],
                    )

            sm[...] = jnp.zeros_like(sm)
            sm[0:6, :] = x_refs[0][0:6, :]
            sm[6:7, :] = column_sum(dq_all[...].astype(F32))
            sm[7:8, :] = column_sum(dv_all[...].astype(F32))
            sm[8:12, :] = x_refs[0][8:12, :]
            sm[12:18, :] = x_refs[1][0:6, :]
            sm[18:20, :] = x_refs[2][0:2, :]
            sm[20:24, :] = x_refs[1][8:12, :]
            sm_low[...] = sm[...].astype(BF)
            engine.load(n_early + n_late - 1, lambda part: sm_low)

        if last:
            def complete_rows(i):
                halo = halo_copies()
                at = block_rows(order[i])
                halo[2 * i].wait_recv()
                halo[2 * i + 1].wait_recv()
                low_ref[at, :] = (g_own[at, :] + one[at, :].astype(F32) + two[at, :].astype(F32)).astype(BF)

        def on(t, when, what, *args):
            @pl.when(t == when)
            def _():
                what(*args)

        def begin(copies):
            for copy in copies:
                copy.start()

        def tick(t, carry):
            @pl.when(t < t_back)
            def _():
                one_block(t)

            on(t, t_back, fetch_w.wait)

            @pl.when((t >= t_back) & (t < t_own))
            def _():
                back_rows(t - t_back)

            @pl.when(t == t_own)
            def _():
                begin(halo_copies())
                fetch_r.wait()

            @pl.when((t >= t_own) & (t < t_weight))
            def _():
                own_rows(t - t_own)

            @pl.when(t == t_weight - 1)
            def _():
                begin(fetch_a)

            @pl.when(t == t_weight)
            def _():
                for copy in fetch_a:
                    copy.wait()

            @pl.when((t >= t_weight) & (t < t_rest))
            def _():
                weight_rows(t - t_weight)

            if last:
                @pl.when(t == t_rest)
                def _():
                    late_pieces()

                @pl.when(t == t_rest + 7)
                def _():
                    complete_rows(0)
                    complete_rows(1)
                    deal(True)
                    memory_copies(True)

            busy = t < t_rest

            @pl.when((t % stride == stride - 1) | jnp.logical_not(busy))
            def _():
                engine.round(jnp.where(busy, t // stride, t - t_rest + t_rest // stride))

            return carry

        lax.fori_loop(0, rounds, tick, 0)
        if not last:
            db_out[0:1, :] = column_sum(dq_all[...].astype(F32))
            db_out[1:2, :] = column_sum(dv_all[...].astype(F32))
            db_out[2:8, :] = jnp.zeros((6, width), F32)
            save = pltpu.make_async_copy(dw, dw_out, loc.at[3])
            save.start()
        engine.finish()
        if last:
            for copy in halo_copies():
                copy.wait_send()
        else:
            save.wait()
            for copy in halo_copies():
                copy.wait()
        deal(False)
        memory_copies(False)

    sums_shape = shape_of((engine.n, engine.rows if last else engine.rows // 8, width), BF)
    blocks_shape = shape_of((2, seg, width), BF)
    memory_shape = shape_of((2, 16, width), BF)
    dma = pltpu.SemaphoreType.DMA
    if last:
        out_shape = [
            sums_shape, blocks_shape, memory_shape, shape_of((n_ready, engine.rows, width), BF),
        ]
        out_specs = [ANY, ANY, ANY, ANY]
        more = [
            pltpu.VMEM((own, width), F32),
            pltpu.VMEM((own, width), BF),
            pltpu.VMEM((own, width), BF),
            pltpu.VMEM((size, width), F32),
            pltpu.VMEM((size, width), BF),
        ]
    else:
        out_shape = [
            sums_shape, blocks_shape, memory_shape,
            shape_of((own, width), F32), shape_of((own, width), BF), shape_of((own, width), BF),
            shape_of((3, width, width), BF), shape_of((8, width), F32),
        ]
        out_specs = [WHOLE, ANY, ANY, WHOLE, ANY, ANY, ANY, WHOLE]
        more = []
    return pl.pallas_call(
        kernel,
        out_shape=out_shape,
        in_specs=[ANY, ANY] + [WHOLE] * 7 + [ANY] + [WHOLE] * n_x + [ANY] * n_e + [WHOLE] * int(last),
        out_specs=out_specs,
        scratch_shapes=[
            pltpu.VMEM(w_in.shape, BF),
            pltpu.VMEM((rows, pair_lanes), F32),
            pltpu.VMEM((rows, pair_lanes), F32),
            pltpu.VMEM((rows, width), BF),
            pltpu.VMEM((rows, width), BF),
            pltpu.VMEM((own, width), BF),
            pltpu.VMEM((back, width), BF),
            pltpu.VMEM((3, width, width), BF),
            dma((5,)), dma((5,)), dma((5,)), dma((2,)), dma((2,)),
        ] + more + engine.scratch(),
        compiler_params=pltpu.CompilerParams(
            collective_id=3 if last else 2, has_side_effects=True, vmem_limit_bytes=62 << 20
        ),
        name="attn_bwd_first" if last else "attn_bwd_second",
    )(a, w_in, q, k, v, do, logs, delta, start_row, dr1, *extra, *early, *([ready] if last else []))


def unpack_sums(parts, runs, shard, width):
    size = min(shard, Sums.height)
    starts = [sum(run[2] for run in runs[:i]) for i in range(len(runs))]
    total = sum(run[2] for run in runs)

    def kernel(*refs):
        ins, outs = refs[:len(parts)], refs[len(parts):len(parts) + 4]
        low, high, s_in, s_out = refs[len(parts) + 4:]

        def fetch(start, run, i):
            part, piece, *_ = run
            return pltpu.make_async_copy(
                ins[part].at[piece + i, pl.ds(0, size)], low.at[start + i], s_in.at[start + i]
            )

        def store(start, run, i):
            *_, o, l, tall = run
            rows = pl.ds(pl.multiple_of(i % tall * size, 8), size)
            lanes = pl.ds(pl.multiple_of(i // tall * width, 128), width) if o in (0, 2) else pl.ds(0, width)
            return pltpu.make_async_copy(high.at[start + i], outs[o].at[l, rows, lanes], s_out.at[start + i])

        def for_all(what):
            for start, run in zip(starts, runs):
                def body(i, carry, start=start, run=run):
                    what(start, run, i)
                    return carry

                lax.fori_loop(0, run[2], body, 0)

        def convert(start, run, i):
            fetch(start, run, i).wait()
            high[start + i] = low[start + i].astype(F32)
            store(start, run, i).start()

        for_all(lambda *job: fetch(*job).start())
        for_all(convert)
        for_all(lambda *job: store(*job).wait())

    return pl.pallas_call(
        kernel,
        in_specs=[ANY] * len(parts),
        out_specs=[ANY] * 4,
        out_shape=[
            shape_of((2, shard, 3 * width), F32),
            shape_of((2, shard, width), F32),
            shape_of((2, shard, 4 * width), F32),
            shape_of((2, 4 * shard, width), F32),
        ],
        scratch_shapes=[
            pltpu.VMEM((total, size, width), BF),
            pltpu.VMEM((total, size, width), F32),
            pltpu.SemaphoreType.DMA((total,)),
            pltpu.SemaphoreType.DMA((total,)),
        ],
        compiler_params=pltpu.CompilerParams(vmem_limit_bytes=VMEM_LIMIT),
        name="unpack_sums",
    )(*parts)


def from_behind(x, axis, by):
    length = lax.axis_size(axis)
    pairs = [(i, i + by) for i in range(length) if 0 <= i + by < length]
    return lax.ppermute(x, axis, pairs)


def local(
    hidden_in, read_memory, doc_ids, cotangent, in_weight, in_bias, out_weight, out_bias, gain_one,
    shift_one, up_weight, up_bias, down_weight, down_bias, gain_two, shift_two,
):
    width = hidden_in.shape[-1]
    seg = cotangent.shape[3]
    mem = read_memory.shape[3]
    own = 2 * seg
    back = 2 * own
    heads = width // HEAD_DIM
    contexts = lax.axis_size("ctx")
    fsdps = lax.axis_size("fsdp")
    place = Place(contexts)
    hidden = up_weight.shape[-1]

    documents = doc_ids[0]
    padded = jnp.concatenate([jnp.full((back,), -1, jnp.int32), documents])
    window_doc = lax.dynamic_slice(padded, (place.chunk * own,), (back + own,))
    query_doc = window_doc[back:]
    start = jnp.sum((window_doc[None, :] < query_doc[:, None]).astype(jnp.int32), axis=1)
    start_col, start_row = start[:, None], start[None, :]

    vectors = [out_bias, gain_one, shift_one, down_bias, gain_two, shift_two]
    six = jnp.stack(vectors, axis=1)
    part = width // fsdps
    packed = jnp.concatenate(
        [six.reshape(2, 6 * part), in_bias, up_bias], axis=1
    ).reshape(-1, 128)

    x0 = jnp.concatenate([read_memory[0, 0], hidden_in[0, 0]], axis=1)
    weights = (in_weight, out_weight, up_weight, down_weight)
    a1, in_1, out_1, up_1, down_1, packed_all = fetch_window(x0, weights, packed, contexts, fsdps, 0)

    packed_all = packed_all.reshape(fsdps, 2, 12 * part).astype(F32)
    six_all = packed_all[:, :, :6 * part].reshape(fsdps, 2, 6, part).transpose(1, 2, 0, 3).reshape(2, 6, 1, width)
    qv_bias = packed_all[:, :, 6 * part:8 * part].transpose(1, 0, 2).reshape(2, 1, 2 * width)
    up_all = packed_all[:, :, 8 * part:].transpose(1, 0, 2).reshape(2, 1, hidden)

    pick_rows = lax.broadcasted_iota(jnp.int32, (heads // 4 * 8, width), 0)
    pick_lane = lax.broadcasted_iota(jnp.int32, (heads // 4 * 8, width), 1) // HEAD_DIM
    pick = ((pick_lane // 4 == pick_rows // 8) & (pick_lane % 4 == pick_rows % 8)).astype(BF)

    def forward(a, h, h_block, w, l):
        w_in, w_out, w_up, w_down = w
        bo, g1, s1, bd, g2, s2 = (six_all[l, i] for i in range(6))
        q, k, v, att, logs = attn_fwd(a, w_in, qv_bias[l], start_col, seg)
        xh1, rs1, mid_low, act, gp, xh2, rs2, out, out_low = ff_fwd(
            att, h, h_block, w_out, w_up, w_down, bo, up_all[l], bd, g1, s1, g2, s2
        )
        return out, out_low, (a, w, l, q, k, v, att, logs, xh1, rs1, mid_low, act, gp, xh2, rs2)

    def backward(grads, saved):
        a, (w_in, w_out, w_up, w_down), l, q, k, v, att, logs, xh1, rs1, mid_low, act, gp, xh2, rs2 = saved
        g1, g2 = six_all[l, 1], six_all[l, 4]
        dwd, dwu, dwo, small, dr1, do, delta = ff_bwd(
            grads, xh2, rs2, g2, gp, act, w_down, w_up, mid_low, xh1, rs1, g1, w_out, att, pick
        )
        delta = delta.reshape(heads // 4, 8, own)
        return small, [dwd, dwu, dwo], (a, w_in, q, k, v, do, logs, delta, start_row, dr1, seg, contexts, fsdps)

    h1, h1_low, saved_1 = forward(a1, a1, 2, (in_1, out_1, up_1, down_1), 0)
    a2, in_2, out_2, up_2, down_2, cot = share_window(h1_low, weights, cotangent[0, 0], contexts, fsdps, 1)
    _, h2_low, saved_2 = forward(a2, h1, 0, (in_2, out_2, up_2, down_2), 1)

    small_2, early_2, state = backward([cot], saved_2)
    scattered, activations, write, g_own, from_one, from_two, dw_2, db_2 = attn_bwd(*state, early_2, (h2_low,))
    small_1, early_1, state = backward([g_own, from_one, from_two], saved_1)
    sums_1, dealt, reads, sums_2 = attn_bwd(
        *state, [dw_2] + early_1, (small_1, small_2, db_2), scattered
    )

    write = write[:, 16 - mem:]
    first = jnp.where(place.me == 0, read_memory[0, 0, 0], write[0])
    new_memory = jnp.stack([first, write[1]])[None, None]
    input_grad = dealt[:, mem:][None, None]
    reads = reads[:, :mem]
    second = jnp.where(place.me == 0, jnp.zeros_like(reads[1]), reads[1])
    memory_grad = jnp.stack([reads[0], second])[None, None]

    shard = width // fsdps

    tall = shard // min(shard, Sums.height)

    def ff_runs(part, first, l):
        return [
            (part, first, 4 * tall, 3, l, 4 * tall),
            (part, first + 4 * tall, 4 * tall, 2, l, tall),
            (part, first + 8 * tall, tall, 1, l, tall),
        ]

    runs = ff_runs(0, 0, 1) + [(1, 0, 3 * tall, 0, 1, tall)] + ff_runs(1, 3 * tall, 0)
    runs.append((1, 12 * tall, 3 * tall, 0, 0, tall))
    in_grad, out_grad, up_grad, down_grad = unpack_sums([sums_2, sums_1], runs, shard, width)

    rows = sums_1[-1, :24].astype(F32).reshape(2, 12, width)
    f = place.f

    def own_part(x):
        size = x.shape[-1] // fsdps
        return lax.dynamic_slice(x, (0, f * size), (2, size))

    dg2, ds2, dbd, dg1, ds1, dbo = (own_part(rows[:, i]) for i in range(6))
    d_in_bias = own_part(rows[:, 6:8].reshape(2, 2 * width))
    d_up_bias = own_part(rows[:, 8:12].reshape(2, hidden))
    return (
        activations[None, None], new_memory, input_grad, memory_grad, in_grad, d_in_bias, out_grad, dbo,
        dg1, ds1, up_grad, d_up_bias, down_grad, dbd, dg2, ds2,
    )


def solution(mesh):
    row = P("fsdp", "ctx", None, None, None)
    mat = P(None, "fsdp", None)
    vec = P(None, "fsdp")
    params = (mat, vec, mat, vec, vec, vec, mat, vec, mat, vec, vec, vec)
    return jax.shard_map(
        local,
        mesh=mesh,
        in_specs=(row, row, P("fsdp", None), row) + params,
        out_specs=(row, row, row, row) + params,
        check_vma=False,
    )
```

time: 3040 us -> 551 us (0.18); the launches traced: 3100 us -> 543 us
  waiting for transfers between devices: 1820 us -> 0 us
  Pallas kernels: 0 us -> 521 us
  local copies, waits for them, and re-layouts: 438 us -> 16.5 us
  matrix products: 339 us -> 0 us
  other arithmetic: 273 us -> 3.11 us
  blocking collectives: 118 us -> 0 us
  loops' own time: 89.3 us -> 0 us
    reduce_scatter x10 -> x0, waiting for transfers between devices: 1020 us -> none  [the longest x2 906 us: backward_layer(): lax.psum_scatter(lax.map(one_piece, (keys_part, values_part, part_pos.res...]
    pallas_call x0 -> x11, Pallas kernels: none -> 521 us  [the longest x2 308 us: attn_bwd(): pl.pallas_call(kernel, out_shape=out_shape, in_specs=[ANY, ANY] + [WHOLE]...]
    all_gather x12 -> x0, waiting for transfers between devices: 503 us -> none  [the longest x2 275 us: forward_layer(): lax.all_gather(mixed_rows[:, 2 * model_width:], 'ctx', axis=0, tiled=True)]
    dot_general x52 -> x0, matrix products: 339 us -> none  [the longest x12 72.9 us: masked_scores(): jnp.einsum('qhd,khd->hqk', query_rows, keys_rows, preferred_element_type=...]
    psum x1 -> x0, waiting for transfers between devices: 290 us -> none  [backward_layer(): lax.psum(shards[0].astype(jnp.bfloat16), 'ctx').astype(jnp.float32)]
    unnamed x254 -> x47, local copies, waits for them, and re-layouts: 131 us -> 9.19 us
    reduce_or x128 -> x0, other arithmetic: 121 us -> none  [the longest x32 31.2 us: query_step(): return (lax.cond(jnp.any(visible), query_update, unchanged, carried), None)]
    dynamic_update_slice x64 -> x0, local copies, waits for them, and re-layouts: 95.5 us -> none  [backward_layer(): lax.map(one_piece, (keys_part, values_part, part_pos.reshape(pieces, piec...]
  transfers between devices with their start and end apart: 27 -> 0, of which waited for: 18 -> 0; matrix products, arithmetic and copies ran while one was open for 18% -> 0% of each run, Pallas kernels for 0% -> 0%
where the time goes in v1:
time: 551 us; the launch traced here: 543 us
  Pallas kernels  521 us (95%)
  local copies, waits for them, and re-layouts  16.5 us (3%)
    pallas_call x2, Pallas kernels, attn_bwd(): pl.pallas_call(kernel, out_shape=out_shape, in_specs=[ANY, ANY] + [WHOLE]...  308 us
    pallas_call x2, Pallas kernels, attn_fwd(): pl.pallas_call(kernel, grid=(steps,), in_specs=[full((rows, width)), pl.B...  55.9 us
    pallas_call x2, Pallas kernels, ff_bwd(): pl.pallas_call(kernel, grid=(steps,), in_specs=[full((own, width))] * cou...  44.5 us
    pallas_call x1, Pallas kernels, share_window(): pl.pallas_call(kernel, out_shape=[shape_of((rows, width), BF)] + full_wei...  35.1 us
    pallas_call x2, Pallas kernels, ff_fwd(): pl.pallas_call(kernel, grid=(steps,), in_specs=[full((own, width)), pl.Bl...  33.7 us
    pallas_call x1, Pallas kernels, fetch_window(): pl.pallas_call(kernel, out_shape=[shape_of((rows, width), BF)] + full_wei...  29.5 us
    pallas_call x1, Pallas kernels, unpack_sums(): pl.pallas_call(kernel, in_specs=[ANY] * len(parts), out_specs=[ANY] * 4,...  15.1 us

profile of v1, /device:TPU:0, one launch (start us, length us, event | category | flops | bytes accessed | tf_op | source)
XLA Modules:
  0.0 542.5 jit_solution(2332823762267164010)
XLA Ops:
  0.6 0.0 copy-start.7
  0.7 0.0 copy-start.8
  0.7 0.0 copy-start.9
  0.7 0.0 copy-start.10
  0.7 0.0 copy-start.11
  0.7 0.0 copy-start.12
  0.7 0.0 copy-start.6
  0.7 0.0 copy-start.5
  0.8 0.8 pad_dynamic-slice_fusion.1
  1.5 0.8 pad_dynamic-slice_fusion
  2.3 0.5 convert_reduce_fusion
  2.8 0.9 copy.51.st_ref
  3.7 0.8 copy.82
  4.4 1.2 copy.75
  5.6 1.1 pad_maximum_fusion.refs_0_
  6.7 0.0 copy-done.8
  6.8 0.0 copy-done.11
  6.9 0.6 reshape.83.refs_5_
  7.5 29.5 %fetch_window.1 = (bf16[1536,768]{1,0:T(8,128)(2,1)}, bf16[768,2304]{1,0:T(8,128)(2,1)}, bf16[768,768]{1,0:T(8,128)(2,1)}, bf16[768,3072]{1,0:T(8,128)(2,1)}, bf...) custom-call(bf16[2,256,768]{2,1,0:T(8,128)(2,1)} %pad_maximum_fusion.refs_0_, bf16[2,384,2304]{2,1,0:T(8,128)(2,1)} %refs_1_.3, ...), custom_call_target="tpu_custom_call" | custom-call | tf_op jit(solution)/shard_map/fetch_window/pallas_call | solution.py:448
  37.0 0.8 reshape.90
  37.8 0.6 fusion.16
  38.4 27.9 %attn_fwd.2 = (bf16[512,768]{1,0:T(8,128)(2,1)}, bf16[1536,768]{1,0:T(8,128)(2,1)}, bf16[1536,768]{1,0:T(8,128)(2,1)}, bf16[512,768]{1,0:T(8,128)(2,1)}, f32[3,8,512]{2,1,0:T(8,128)}) custom-call(bf16[1536,768]{1,0:T(8,128)(2,1)} %get-tuple-element.85.a_ref.h_ref.refs_0_, bf16[768,2304]{1,0:T(8,128)(2,1)} %get-tuple-element.86.wq.wk.wv.refs_1_, ...), custom_call_target="tpu_custom_call" | custom-call | tf_op jit(solution)/shard_map/attn_fwd/pallas_call | solution.py:117
  66.4 0.6 slice_bitcast_fusion.6
  67.1 0.6 fusion.15
  67.7 16.6 %ff_fwd.2 = (f32[512,768]{1,0:T(8,128)}, f32[512,1]{1,0:T(8,128)}, bf16[512,768]{1,0:T(8,128)(2,1)}, bf16[512,3072]{1,0:T(8,128)(2,1)}, bf16[512,3072]{1,0:T(8,1...) custom-call(bf16[512,768]{1,0:T(8,128)(2,1)} %get-tuple-element.88.att_ref.refs, ...), custom_call_target="tpu_custom_call" | custom-call | tf_op jit(solution)/shard_map/ff_fwd/pallas_call | solution.py:196
  84.4 35.1 %share_window.1 = (bf16[1536,768]{1,0:T(8,128)(2,1)}, bf16[768,2304]{1,0:T(8,128)(2,1)}, bf16[768,768]{1,0:T(8,128)(2,1)}, bf16[768,3072]{1,0:T(8,128)(2,1)}, bf...) custom-call(bf16[512,768]{1,0:T(8,128)(2,1)} %get-tuple-element.92.refs_0_, bf16[2,384,2304]{2,1,0:T(8,128)(2,1)} %refs_1_.3, ...), custom_call_target="tpu_custom_call" | custom-call | tf_op jit(solution)/shard_map/share_window/pallas_call | solution.py:513
  119.4 28.0 %attn_fwd.3 = (bf16[512,768]{1,0:T(8,128)(2,1)}, bf16[1536,768]{1,0:T(8,128)(2,1)}, bf16[1536,768]{1,0:T(8,128)(2,1)}, bf16[512,768]{1,0:T(8,128)(2,1)}, f32[3,8,512]{2,1,0:T(8,128)}) custom-call(bf16[1536,768]{1,0:T(8,128)(2,1)} %get-tuple-element.93.a_ref.refs_0_, bf16[768,2304]{1,0:T(8,128)(2,1)} %get-tuple-element.94.wq.wk.wv.refs_1_, ...), custom_call_target="tpu_custom_call" | custom-call | tf_op jit(solution)/shard_map/attn_fwd/pallas_call | solution.py:117
  147.5 17.1 %ff_fwd.3 = (f32[512,768]{1,0:T(8,128)}, f32[512,1]{1,0:T(8,128)}, bf16[512,768]{1,0:T(8,128)(2,1)}, bf16[512,3072]{1,0:T(8,128)(2,1)}, bf16[512,3072]{1,0:T(8,1...) custom-call(bf16[512,768]{1,0:T(8,128)(2,1)} %get-tuple-element.99.att_ref.refs, ...), custom_call_target="tpu_custom_call" | custom-call | tf_op jit(solution)/shard_map/ff_fwd/pallas_call | solution.py:196
  164.6 0.7 fusion.7.refs_14_.refs_16_
  165.3 21.8 %ff_bwd.2 = (bf16[3072,768]{1,0:T(8,128)(2,1)}, bf16[768,3072]{1,0:T(8,128)(2,1)}, bf16[768,768]{1,0:T(8,128)(2,1)}, f32[16,768]{1,0:T(8,128)}, f32[512,768]{1,0...) custom-call(bf16[512,768]{1,0:T(8,128)(2,1)} %get-tuple-element.98.refs_0_, ...), custom_call_target="tpu_custom_call" | custom-call | tf_op jit(solution)/shard_map/ff_bwd/pallas_call | solution.py:306
  187.1 83.3 %attn_bwd_second.1 = (bf16[27,16,768]{2,1,0:T(8,128)(2,1)}, bf16[2,256,768]{2,1,0:T(8,128)(2,1)}, bf16[2,16,768]{2,1,0:T(8,128)(2,1)}, f32[512,768]{1,0:T(8,128)...) custom-call(bf16[1536,768]{1,0:T(8,128)(2,1)} %get-tuple-element.93.a_r, ...), custom_call_target="tpu_custom_call" | custom-call | tf_op jit(solution)/shard_map/attn_bwd_second/pallas_call | solution.py:1326
  270.4 22.6 %ff_bwd.3 = (bf16[3072,768]{1,0:T(8,128)(2,1)}, bf16[768,3072]{1,0:T(8,128)(2,1)}, bf16[768,768]{1,0:T(8,128)(2,1)}, f32[16,768]{1,0:T(8,128)}, f32[512,768]{1,0...) custom-call(f32[512,768]{1,0:T(8,128)} %get-tuple-element.124.refs_0_, ...), custom_call_target="tpu_custom_call" | custom-call | tf_op jit(solution)/shard_map/ff_bwd/pallas_call | solution.py:306
  293.0 224.4 %attn_bwd_first.1 = (bf16[46,128,768]{2,1,0:T(8,128)(2,1)}, bf16[2,256,768]{2,1,0:T(8,128)(2,1)}, bf16[2,16,768]{2,1,0:T(8,128)(2,1)}, bf16[27,128,768]{2,1,0:T(8,128)(2,1)}) custom-call(bf16[1536,768]{1,0:T(8,128)(2,1)} %get-tuple-element.85.a_ref.h_ref.refs_0_, bf16[768,2304]{1,0:T(8,128)(2,1)} %get-tuple-element.86.wq.wk.wv.refs_1_, ...), custom_call_target="tpu_custom_call" | custom-call | tf_op jit(solution)/shard_map/attn_bwd_first/pallas_call | solution.py:1326
  517.5 15.1 %unpack_sums.1 = (f32[2,384,2304]{2,1,0:T(8,128)}, f32[2,384,768]{2,1,0:T(8,128)}, f32[2,384,3072]{2,1,0:T(8,128)}, f32[2,1536,768]{2,1,0:T(8,128)}) custom-call(bf16[27,128,768]{2,1,0:T(8,128)(2,1)} %get-tuple-element.148.refs_0_, bf16[46,128,768]{2,1,0:T(8,128)(2,1)} %get-tuple-element.149.refs_1_), custom_call_target="tpu_custom_call" | custom-call | tf_op jit(solution)/shard_map/unpack_sums/pallas_call | solution.py:1387
  532.7 0.6 copy.57
  533.3 0.2 slice_bitcast_fusion
  533.5 1.5 copy.56
  534.9 0.8 slice_convert_fusion
  535.8 0.6 constant_dynamic-slice_fusion.3
  536.4 0.6 copy.76
  537.0 0.6 copy.77
  537.6 0.6 copy.78
  538.2 0.6 copy.79
  538.8 0.6 copy.80
  539.3 0.6 copy.81
  539.9 0.6 constant_dynamic-slice_fusion.7
  540.6 0.6 copy.55
  541.2 0.9 copy.89
  (50 shorter events, 0.4 us)
Async XLA Ops:
  0.6 6.0 %copy-start.7 = (bf16[2,384]{1,0:T(2,128)(2,1)S(1)}, bf16[2,384]{1,0:T(2,128)(2,1)}, u32[]{:S(2)}) copy-start(bf16[2,384]{1,0:T(2,128)(2,1)} %param.23) | copy-start | bytes 4612
  0.7 6.0 %copy-start.8 = (bf16[2,384]{1,0:T(2,128)(2,1)S(1)}, bf16[2,384]{1,0:T(2,128)(2,1)}, u32[]{:S(2)}) copy-start(bf16[2,384]{1,0:T(2,128)(2,1)} %param.24) | copy-start | bytes 4612
  0.7 6.0 %copy-start.9 = (bf16[2,384]{1,0:T(2,128)(2,1)S(1)}, bf16[2,384]{1,0:T(2,128)(2,1)}, u32[]{:S(2)}) copy-start(bf16[2,384]{1,0:T(2,128)(2,1)} %param.25) | copy-start | bytes 4612
  0.7 6.1 %copy-start.10 = (bf16[2,384]{1,0:T(2,128)(2,1)S(1)}, bf16[2,384]{1,0:T(2,128)(2,1)}, u32[]{:S(2)}) copy-start(bf16[2,384]{1,0:T(2,128)(2,1)} %param.29) | copy-start | bytes 4612
  0.7 6.1 %copy-start.11 = (bf16[2,384]{1,0:T(2,128)(2,1)S(1)}, bf16[2,384]{1,0:T(2,128)(2,1)}, u32[]{:S(2)}) copy-start(bf16[2,384]{1,0:T(2,128)(2,1)} %param.30) | copy-start | bytes 4612
  0.7 6.1 %copy-start.12 = (bf16[2,384]{1,0:T(2,128)(2,1)S(1)}, bf16[2,384]{1,0:T(2,128)(2,1)}, u32[]{:S(2)}) copy-start(bf16[2,384]{1,0:T(2,128)(2,1)} %param.31) | copy-start | bytes 4612
  0.7 6.1 %copy-start.6 = (bf16[2,768]{1,0:T(2,128)(2,1)S(1)}, bf16[2,768]{1,0:T(2,128)(2,1)}, u32[]{:S(2)}) copy-start(bf16[2,768]{1,0:T(2,128)(2,1)} %param.21) | copy-start | bytes 9220
  0.7 6.1 %copy-start.5 = (bf16[2,1536]{1,0:T(2,128)(2,1)S(1)}, bf16[2,1536]{1,0:T(2,128)(2,1)}, u32[]{:S(2)}) copy-start(bf16[2,1536]{1,0:T(2,128)(2,1)} %param.27) | copy-start | bytes 18436
  2.8 34.2 %copy-start.4 = (s32[512]{0:T(512)}, s32[512]{0:T(512)S(1)}, u32[]{:S(2)}) copy-start(s32[512]{0:T(512)S(1)} %convert_reduce_fusion) | copy-start | bytes 6148
  517.5 15.2 %copy-start.2 = (bf16[2,16,768]{2,1,0:T(8,128)(2,1)S(1)}, bf16[2,16,768]{2,1,0:T(8,128)(2,1)}, u32[]{:S(2)}) copy-start(bf16[2,16,768]{2,1,0:T(8,128)(2,1)} %get-tuple-element.147) | copy-start | bytes 147460
  517.5 15.8 %copy-start.1 = (bf16[2,256,768]{2,1,0:T(8,128)(2,1)S(1)}, bf16[2,256,768]{2,1,0:T(8,128)(2,1)}, u32[]{:S(2)}) copy-start(bf16[2,256,768]{2,1,0:T(8,128)(2,1)} %get-tuple-element.146) | copy-start | bytes 2359300
  532.6 8.0 %copy-start.3 = (bf16[2,16,768]{2,1,0:T(8,128)(2,1)S(1)}, bf16[2,16,768]{2,1,0:T(8,128)(2,1)}, u32[]{:S(2)}) copy-start(bf16[2,16,768]{2,1,0:T(8,128)(2,1)} %get-tuple-element.120) | copy-start | bytes 147460
  532.6 8.6 %copy-start = (bf16[2,256,768]{2,1,0:T(8,128)(2,1)S(1)}, bf16[2,256,768]{2,1,0:T(8,128)(2,1)}, u32[]{:S(2)}) copy-start(bf16[2,256,768]{2,1,0:T(8,128)(2,1)} %get-tuple-element.119) | copy-start | bytes 2359300
